TPU v7x, 32 devices: a whole 2x2x4 slice. The times are simulated.
32 devices in a mesh: fsdp: 16 (over z, y, x), dp: 2 (over core).
Axes of the slice: x: 2, y: 2, z: 4, core: 2. Of those that a mesh axis runs over, the one named last changes fastest.
Arguments:
- tokens: bfloat16 [64, 384, 768], P(('fsdp', 'dp')), may hold values from -6 to 6
- segments: int32 [64, 384], P(('fsdp', 'dp')), may hold values from 0 to 4, never falling along the last dimension, each value on 1 to 360 neighbouring positions
- first_gain: bfloat16 [768], P('fsdp'), may hold values from 0.5 to 1.5
- first_shift: bfloat16 [768], P('fsdp'), may hold values from -1 to 1
- qkv_weight: bfloat16 [768, 2304], P('fsdp'), may hold values from -0.21875 to 0.21875
- query_bias: bfloat16 [768], P('fsdp'), may hold values from -1 to 1
- value_bias: bfloat16 [768], P('fsdp'), may hold values from -1 to 1
- out_weight: bfloat16 [768, 768], P('fsdp'), may hold values from -0.875 to 0.875
- out_bias: bfloat16 [768], P('fsdp'), may hold values from -1 to 1
- second_gain: bfloat16 [768], P('fsdp'), may hold values from 0.5 to 1.5
- second_shift: bfloat16 [768], P('fsdp'), may hold values from -1 to 1
- up_weight: bfloat16 [768, 3072], P('fsdp'), may hold values from -0.21875 to 0.21875
- up_bias: bfloat16 [3072], P('fsdp'), may hold values from -1 to 1
- down_weight: bfloat16 [3072, 768], P('fsdp'), may hold values from -0.109375 to 0.109375
- down_bias: bfloat16 [768], P('fsdp'), may hold values from -1 to 1
- cotangent: bfloat16 [64, 384, 768], P(('fsdp', 'dp')), may hold values from -6 to 6
Outputs:
- layer_out: bfloat16 [64, 384, 768], P(('fsdp', 'dp'))
- tokens_grad: float32 [64, 384, 768], P(('fsdp', 'dp'))
- first_gain_grad: float32 [768], P(('fsdp', 'dp'))
- first_shift_grad: float32 [768], P(('fsdp', 'dp'))
- qkv_weight_grad: float32 [768, 2304], P(('fsdp', 'dp'))
- query_bias_grad: float32 [768], P(('fsdp', 'dp'))
- value_bias_grad: float32 [768], P(('fsdp', 'dp'))
- out_weight_grad: float32 [768, 768], P(('fsdp', 'dp'))
- out_bias_grad: float32 [768], P(('fsdp', 'dp'))
- second_gain_grad: float32 [768], P(('fsdp', 'dp'))
- second_shift_grad: float32 [768], P(('fsdp', 'dp'))
- up_weight_grad: float32 [768, 3072], P(('fsdp', 'dp'))
- up_bias_grad: float32 [3072], P(('fsdp', 'dp'))
- down_weight_grad: float32 [3072, 768], P(('fsdp', 'dp'))
- down_bias_grad: float32 [768], P(('fsdp', 'dp'))
Inputs may be any that keep to these rules, and one draw needn't show every extreme that they name: `segments`: segment numbers never fall along a sequence; an image holds 1 to 360 patches.
All inputs are finite; a program needn't handle non-finite values.
Results may differ from a plain program's by a relative error of at most 0.015.
Values may be sent and summed in bfloat16 or wider, within the bound.
A program may use at most 192 MiB of HBM per device.

v0:
```python
import math

import jax
import jax.numpy as jnp
from jax import lax
from jax.sharding import PartitionSpec as P

HEADS = 12


EPSILON = 1e-06
SLOPE = math.sqrt(2.0 / math.pi)
CUBIC = 0.044715


def product(left_side, right_side):
    return jnp.dot(left_side, right_side, preferred_element_type=jnp.float32)


def product_left_turned(left_side, right_side):
    return lax.dot_general(
        left_side, right_side, (((0,), (0,)), ((), ())), preferred_element_type=jnp.float32
    )


def product_right_turned(left_side, right_side):
    return lax.dot_general(
        left_side, right_side, (((1,), (1,)), ((), ())), preferred_element_type=jnp.float32
    )


def norm_forward(features, norm_gain, norm_shift):
    centered = features - jnp.mean(features, axis=-1, keepdims=True)
    inv_spread = lax.rsqrt(jnp.mean(centered * centered, axis=-1, keepdims=True) + EPSILON)
    unit_rows = centered * inv_spread
    return (unit_rows * norm_gain + norm_shift, unit_rows, inv_spread)


def norm_backward(grad_normed, unit_rows, inv_spread, norm_gain):
    scaled = grad_normed * norm_gain
    inner = (
        scaled
        - jnp.mean(scaled, axis=-1, keepdims=True)
        - unit_rows * jnp.mean(scaled * unit_rows, axis=-1, keepdims=True)
    )
    return (
        inner * inv_spread,
        jnp.sum(grad_normed * unit_rows, axis=0),
        jnp.sum(grad_normed, axis=0),
    )


def smooth_gate(features):
    return (
        0.5
        * features
        * (1.0 + jnp.tanh(SLOPE * (features + CUBIC * features * features * features)))
    )


def gate_slope(features):
    bent = jnp.tanh(SLOPE * (features + CUBIC * features * features * features))
    return 0.5 * (1.0 + bent) + 0.5 * features * (1.0 - bent * bent) * SLOPE * (
        1.0 + 3.0 * CUBIC * features * features
    )


def masked_scores(queries, key_rows, same_image, score_scale):
    scores = (
        jnp.einsum("qhd,khd->hqk", queries, key_rows, preferred_element_type=jnp.float32)
        * score_scale
    )
    return jnp.where(same_image[None], scores, -1e30)


def attend_forward(queries, key_rows, values, same_image, score_scale):
    step_heads = queries.shape[1] // 4
    outputs = []
    totals = []
    for head_block in range(4):
        head_span = slice(head_block * step_heads, (head_block + 1) * step_heads)
        scores = masked_scores(
            queries[:, head_span], key_rows[:, head_span], same_image, score_scale
        )
        row_top = jnp.max(scores, axis=-1, keepdims=True)
        exponent = jnp.exp(scores - row_top)
        row_total = jnp.sum(exponent, axis=-1, keepdims=True)
        weights_low = (exponent / row_total).astype(jnp.bfloat16)
        outputs.append(
            jnp.einsum(
                "hqk,khd->qhd",
                weights_low,
                values[:, head_span],
                preferred_element_type=jnp.float32,
            )
        )
        totals.append(row_top + jnp.log(row_total))
    return (jnp.concatenate(outputs, axis=1), totals)


def attend_backward(queries, key_rows, values, same_image, score_scale, totals, grad_attended):
    step_heads = queries.shape[1] // 4
    query_parts = []
    key_parts = []
    value_parts = []
    for head_block in range(4):
        head_span = slice(head_block * step_heads, (head_block + 1) * step_heads)
        scores = masked_scores(
            queries[:, head_span], key_rows[:, head_span], same_image, score_scale
        )
        probability = jnp.exp(scores - totals[head_block])
        grad_piece = grad_attended[:, head_span]
        grad_values = jnp.einsum(
            "hqk,qhd->khd",
            probability.astype(jnp.bfloat16),
            grad_piece,
            preferred_element_type=jnp.float32,
        )
        grad_probs = jnp.einsum(
            "qhd,khd->hqk", grad_piece, values[:, head_span], preferred_element_type=jnp.float32
        )
        grad_scores = (
            probability * (grad_probs - jnp.sum(grad_probs * probability, axis=-1, keepdims=True))
        ).astype(jnp.bfloat16)
        grad_queries = (
            jnp.einsum(
                "hqk,khd->qhd",
                grad_scores,
                key_rows[:, head_span],
                preferred_element_type=jnp.float32,
            )
            * score_scale
        )
        grad_keys = (
            jnp.einsum(
                "hqk,qhd->khd",
                grad_scores,
                queries[:, head_span],
                preferred_element_type=jnp.float32,
            )
            * score_scale
        )
        query_parts.append(grad_queries.astype(jnp.bfloat16))
        key_parts.append(grad_keys.astype(jnp.bfloat16))
        value_parts.append(grad_values.astype(jnp.bfloat16))
    return (
        jnp.concatenate(query_parts, axis=1),
        jnp.concatenate(key_parts, axis=1),
        jnp.concatenate(value_parts, axis=1),
    )


def per_device(
    tokens,
    segments,
    first_gain,
    first_shift,
    qkv_weight,
    query_bias,
    value_bias,
    out_weight,
    out_bias,
    second_gain,
    second_shift,
    up_weight,
    up_bias,
    down_weight,
    down_bias,
    cotangent,
):
    head_count = HEADS
    model_width = tokens.shape[2]
    head_width = model_width // head_count
    score_scale = 1.0 / math.sqrt(head_width)
    gain_one, shift_one, qkv_full, query_shift, value_shift, out_full, out_shift = (
        lax.all_gather(first_gain, "fsdp", axis=0, tiled=True),
        lax.all_gather(first_shift, "fsdp", axis=0, tiled=True),
        lax.all_gather(qkv_weight, "fsdp", axis=0, tiled=True),
        lax.all_gather(query_bias, "fsdp", axis=0, tiled=True),
        lax.all_gather(value_bias, "fsdp", axis=0, tiled=True),
        lax.all_gather(out_weight, "fsdp", axis=0, tiled=True),
        lax.all_gather(out_bias, "fsdp", axis=0, tiled=True),
    )
    gain_two, shift_two, up_full, up_shift, down_full, down_shift = (
        lax.all_gather(second_gain, "fsdp", axis=0, tiled=True),
        lax.all_gather(second_shift, "fsdp", axis=0, tiled=True),
        lax.all_gather(up_weight, "fsdp", axis=0, tiled=True),
        lax.all_gather(up_bias, "fsdp", axis=0, tiled=True),
        lax.all_gather(down_weight, "fsdp", axis=0, tiled=True),
        lax.all_gather(down_bias, "fsdp", axis=0, tiled=True),
    )
    first_scale = gain_one.astype(jnp.float32)
    first_offset = shift_one.astype(jnp.float32)
    second_scale = gain_two.astype(jnp.float32)
    second_offset = shift_two.astype(jnp.float32)
    query_offset = query_shift.astype(jnp.float32)
    value_offset = value_shift.astype(jnp.float32)
    out_offset = out_shift.astype(jnp.float32)
    up_offset = up_shift.astype(jnp.float32)
    down_offset = down_shift.astype(jnp.float32)
    micro_count = tokens.shape[0]
    saved = []
    outputs_low = []
    for batch_index in range(micro_count):
        inputs = tokens[batch_index].astype(jnp.float32)
        segment_row = segments[batch_index]
        same_image = segment_row[:, None] == segment_row[None, :]
        normed, unit_one, spread_one = norm_forward(inputs, first_scale, first_offset)
        normed_low = normed.astype(jnp.bfloat16)
        mixed_qkv = product(normed_low, qkv_full)
        queries = (
            (mixed_qkv[:, :model_width] + query_offset)
            .astype(jnp.bfloat16)
            .reshape(-1, head_count, head_width)
        )
        key_rows = (
            mixed_qkv[:, model_width : 2 * model_width]
            .astype(jnp.bfloat16)
            .reshape(-1, head_count, head_width)
        )
        values = (
            (mixed_qkv[:, 2 * model_width :] + value_offset)
            .astype(jnp.bfloat16)
            .reshape(-1, head_count, head_width)
        )
        attended, totals = attend_forward(queries, key_rows, values, same_image, score_scale)
        attended_low = attended.reshape(-1, model_width).astype(jnp.bfloat16)
        hidden = inputs + (product(attended_low, out_full) + out_offset)
        normed_two, unit_two, spread_two = norm_forward(hidden, second_scale, second_offset)
        normed_two_low = normed_two.astype(jnp.bfloat16)
        upward = product(normed_two_low, up_full) + up_offset
        active_low = smooth_gate(upward).astype(jnp.bfloat16)
        result = hidden + (product(active_low, down_full) + down_offset)
        outputs_low.append(result.astype(jnp.bfloat16))
        saved.append(
            (
                same_image,
                unit_one,
                spread_one,
                normed_low,
                queries,
                key_rows,
                values,
                totals,
                attended_low,
                unit_two,
                spread_two,
                normed_two_low,
                upward,
                active_low,
            )
        )
    gain_two_back, up_back, down_back = (
        lax.all_gather(second_gain, "fsdp", axis=0, tiled=True),
        lax.all_gather(up_weight, "fsdp", axis=0, tiled=True),
        lax.all_gather(down_weight, "fsdp", axis=0, tiled=True),
    )
    gain_one_back, qkv_back, out_back = (
        lax.all_gather(first_gain, "fsdp", axis=0, tiled=True),
        lax.all_gather(qkv_weight, "fsdp", axis=0, tiled=True),
        lax.all_gather(out_weight, "fsdp", axis=0, tiled=True),
    )
    first_scale_back = gain_one_back.astype(jnp.float32)
    second_scale_back = gain_two_back.astype(jnp.float32)
    accum = [
        jnp.zeros(item_array.shape, jnp.float32)
        for item_array in (
            gain_one,
            shift_one,
            qkv_full,
            query_shift,
            value_shift,
            out_full,
            out_shift,
            gain_two,
            shift_two,
            up_full,
            up_shift,
            down_full,
            down_shift,
        )
    ]
    grads_back = []
    for batch_index in range(micro_count):
        (
            same_image,
            unit_one,
            spread_one,
            normed_low,
            queries,
            key_rows,
            values,
            totals,
            attended_low,
            unit_two,
            spread_two,
            normed_two_low,
            upward,
            active_low,
        ) = saved[batch_index]
        grad_down = cotangent[batch_index]
        grad_top = grad_down.astype(jnp.float32)
        down_term = product_left_turned(active_low, grad_down)
        grad_active = product_right_turned(grad_down, down_back)
        grad_up = (grad_active * gate_slope(upward)).astype(jnp.bfloat16)
        up_term = product_left_turned(normed_two_low, grad_up)
        grad_normed_two = product_right_turned(grad_up, up_back)
        hidden_part, gain_two_term, shift_two_term = norm_backward(
            grad_normed_two, unit_two, spread_two, second_scale_back
        )
        grad_hidden = grad_top + hidden_part
        grad_branch = grad_hidden.astype(jnp.bfloat16)
        out_term = product_left_turned(attended_low, grad_branch)
        grad_attended = (
            product_right_turned(grad_branch, out_back)
            .astype(jnp.bfloat16)
            .reshape(-1, head_count, head_width)
        )
        grad_queries, grad_keys, grad_values = attend_backward(
            queries, key_rows, values, same_image, score_scale, totals, grad_attended
        )
        grad_queries = grad_queries.reshape(-1, model_width)
        grad_keys = grad_keys.reshape(-1, model_width)
        grad_values = grad_values.reshape(-1, model_width)
        grad_mixed = jnp.concatenate([grad_queries, grad_keys, grad_values], axis=1)
        qkv_term = product_left_turned(normed_low, grad_mixed)
        grad_normed = product_right_turned(grad_mixed, qkv_back)
        input_part, gain_one_term, shift_one_term = norm_backward(
            grad_normed, unit_one, spread_one, first_scale_back
        )
        grads_back.append(grad_hidden + input_part)
        terms = (
            gain_one_term,
            shift_one_term,
            qkv_term,
            jnp.sum(grad_queries.astype(jnp.float32), axis=0),
            jnp.sum(grad_values.astype(jnp.float32), axis=0),
            out_term,
            jnp.sum(grad_branch.astype(jnp.float32), axis=0),
            gain_two_term,
            shift_two_term,
            up_term,
            jnp.sum(grad_up.astype(jnp.float32), axis=0),
            down_term,
            jnp.sum(grad_top, axis=0),
        )
        accum = [earlier + later for earlier, later in zip(accum, terms)]
    shares = (
        lax.psum_scatter(accum[0], ("fsdp", "dp"), scatter_dimension=0, tiled=True),
        lax.psum_scatter(accum[1], ("fsdp", "dp"), scatter_dimension=0, tiled=True),
        lax.psum_scatter(accum[2], ("fsdp", "dp"), scatter_dimension=0, tiled=True),
        lax.psum_scatter(accum[3], ("fsdp", "dp"), scatter_dimension=0, tiled=True),
        lax.psum_scatter(accum[4], ("fsdp", "dp"), scatter_dimension=0, tiled=True),
        lax.psum_scatter(accum[5], ("fsdp", "dp"), scatter_dimension=0, tiled=True),
        lax.psum_scatter(accum[6], ("fsdp", "dp"), scatter_dimension=0, tiled=True),
        lax.psum_scatter(accum[7], ("fsdp", "dp"), scatter_dimension=0, tiled=True),
        lax.psum_scatter(accum[8], ("fsdp", "dp"), scatter_dimension=0, tiled=True),
        lax.psum_scatter(accum[9], ("fsdp", "dp"), scatter_dimension=0, tiled=True),
        lax.psum_scatter(accum[10], ("fsdp", "dp"), scatter_dimension=0, tiled=True),
        lax.psum_scatter(accum[11], ("fsdp", "dp"), scatter_dimension=0, tiled=True),
        lax.psum_scatter(accum[12], ("fsdp", "dp"), scatter_dimension=0, tiled=True),
    )
    return (
        jnp.stack(outputs_low),
        jnp.stack(grads_back),
        shares[0],
        shares[1],
        shares[2],
        shares[3],
        shares[4],
        shares[5],
        shares[6],
        shares[7],
        shares[8],
        shares[9],
        shares[10],
        shares[11],
        shares[12],
    )


def solution(mesh):
    in_specs = (
        P(("fsdp", "dp"), None, None),
        P(("fsdp", "dp"), None),
        P("fsdp"),
        P("fsdp"),
        P("fsdp", None),
        P("fsdp"),
        P("fsdp"),
        P("fsdp", None),
        P("fsdp"),
        P("fsdp"),
        P("fsdp"),
        P("fsdp", None),
        P("fsdp"),
        P("fsdp", None),
        P("fsdp"),
        P(("fsdp", "dp"), None, None),
    )
    out_specs = (
        P(("fsdp", "dp"), None, None),
        P(("fsdp", "dp"), None, None),
        P(("fsdp", "dp")),
        P(("fsdp", "dp")),
        P(("fsdp", "dp"), None),
        P(("fsdp", "dp")),
        P(("fsdp", "dp")),
        P(("fsdp", "dp"), None),
        P(("fsdp", "dp")),
        P(("fsdp", "dp")),
        P(("fsdp", "dp")),
        P(("fsdp", "dp"), None),
        P(("fsdp", "dp")),
        P(("fsdp", "dp"), None),
        P(("fsdp", "dp")),
    )
    return jax.shard_map(
        per_device, mesh=mesh, in_specs=in_specs, out_specs=out_specs, check_vma=False
    )
```

profile of v0, /device:TPU:0, one launch (start us, length us, event | category | flops | bytes accessed | tf_op | source)
XLA Modules:
  0.0 893.4 jit_solution(10122971592221002491)
XLA Ops:
  17.6 79.5 %all-reduce.19 = (bf16[768]{0:T(1024)(128)(2,1)S(1)}, bf16[768]{0:T(1024)(128)(2,1)S(1)}, bf16[768]{0:T(1024)(128)(2,1)S(1)}, bf16[768]{0:T(1024)(128)(2,1)S(1)}...) all-reduce(bf16[768]{0:T(1024)(128)(2,1)S(1)} %dynamic-update-slice, ...), channel_id=1, replica_groups=mesh['fsdp'=16,'dp'=2] {'fsdp'}, use_global_device_ids=true, to_apply=%add.1 | all-reduce | flops 9216 | bytes 36864
  99.3 3.8 fusion.187
  108.1 3.9 fusion.70
  112.3 2.4 fusion.195
  114.7 2.3 fusion.196
  144.0 2.5 fusion.199
  155.8 69.9 %all-gather.9.cloned.1.call-done = bf16[768,3072]{1,0:T(8,128)(2,1)} async-done(((bf16[48,3072]{1,0:T(8,128)(2,1)}), bf16[768,3072]{1,0:T(8,128)(2,1)}) %all-gather.9.cloned.1.call-update) | async-done | bytes 4718608 | tf_op jit(solution)/shard_map/all_gather | solution.py:187
  225.6 6.9 convolution_add_fusion.3
  232.5 74.9 %all-gather.11.cloned.1.call-done = bf16[3072,768]{1,0:T(8,128)(2,1)} async-done(((bf16[192,768]{1,0:T(8,128)(2,1)}), bf16[3072,768]{1,0:T(8,128)(2,1)}) %all-gather.11.cloned.1.call-update) | async-done | bytes 4718608 | tf_op jit(solution)/shard_map/all_gather | solution.py:189
  307.4 7.5 convert_reduce_fusion
  319.4 5.1 convert_reduce_fusion.1
  324.5 3.2 multiply_reduce_fusion.9
  327.7 2.9 convert_reduce_fusion.2
  335.3 2.7 fusion.105
  360.7 2.7 fusion.101
  363.4 3.4 multiply_reduce_fusion.4
  368.0 2.3 multiply_reduce_fusion.5
  374.8 2.5 multiply_reduce_fusion.7
  379.8 2.5 multiply_convert_fusion.6
  395.2 5.3 convolution_add_fusion
  401.8 5.1 fusion.143
  407.0 9.3 %convolution_add_fusion.1 = f32[3072,768]{1,0:T(8,128)} fusion(f32[3072,768]{1,0:T(8,128)S(1)} %fusion.143, bf16[2,384,768]{2,1,0:T(8,128)(2,1)S(1)} %copy-done.45, f32[384,3072]{1,0:T(8,128)} %convolution_add_fusion.3), kind=kOutput, calls=%fused_computation.5 | convolution fusion | flops 1824915456 | bytes 24182784 | tf_op jit(solution)/shard_map/dot_general | solution.py:21
  417.6 4.7 fusion.189
  422.3 6.0 convolution_add_fusion.2
  440.1 4.3 fusion.138
  444.5 4.0 fusion.68
  449.8 41.3 %all-reduce.18 = (f32[768]{0:T(1024)}, f32[768]{0:T(1024)}, f32[768]{0:T(1024)}, f32[768]{0:T(1024)}, f32[768]{0:T(1024)}, /*index=5*/f32[768]{0:T(1024)}, f32[768]{0:T(1024)}, f32[3072]{0:T(1024)}, f32[768]{0:T(1024)}) all-reduce(f32[768]{0:T(1024)} %add.366, f32[768]{0:T(1024)} %add.367, ...), channel_id=2, replica_groups=mesh['fsdp'=16,'dp'=2] {'fsdp','dp'}, use_global_device_ids=true, to_apply=%region_42.43.clone | all-reduce | flops 9216 | bytes 73728
  502.5 6.9 fusion.51
  509.4 7.1 fusion.50
  521.2 81.7 %reduce-scatter.5.cloned.1.call-done = f32[24,2304]{1,0:T(8,128)} async-done(((f32[768,2304]{1,0:T(8,128)}), f32[24,2304]{1,0:T(8,128)}) %reduce-scatter.5.cloned.1.call-update) | async-done | bytes 221200 | tf_op jit(solution)/shard_map/reduce_scatter | solution.py:351
  602.9 141.4 %reduce-scatter.11.cloned.1.call-done = f32[96,768]{1,0:T(8,128)} async-done(((f32[3072,768]{1,0:T(8,128)}), f32[96,768]{1,0:T(8,128)}) %reduce-scatter.11.cloned.1.call-update) | async-done | bytes 294928 | tf_op jit(solution)/shard_map/reduce_scatter | solution.py:360
  744.3 142.1 %reduce-scatter.9.cloned.1.call-done = f32[24,3072]{1,0:T(8,128)} async-done(((f32[768,3072]{1,0:T(8,128)}), f32[24,3072]{1,0:T(8,128)}) %reduce-scatter.9.cloned.1.call-update) | async-done | bytes 294928 | tf_op jit(solution)/shard_map/reduce_scatter | solution.py:358
  (545 shorter events, 135.4 us)
Async XLA Ops:
  7.2 7.8 copy-start.20
  7.2 8.3 copy-start.169
  7.2 8.5 copy-start.170
  7.2 8.8 copy-start.171
  7.2 9.0 %copy-start.172 = (bf16[48]{0:T(256)(128)(2,1)S(1)}, bf16[48]{0:T(256)(128)(2,1)}, u32[]{:S(2)}) copy-start(bf16[48]{0:T(256)(128)(2,1)} %param.21) | copy-start | bytes 292
  7.2 9.2 %copy-start.173 = (bf16[48]{0:T(256)(128)(2,1)S(1)}, bf16[48]{0:T(256)(128)(2,1)}, u32[]{:S(2)}) copy-start(bf16[48]{0:T(256)(128)(2,1)} %param.22) | copy-start | bytes 292
  7.2 9.4 %copy-start.174 = (bf16[48]{0:T(256)(128)(2,1)S(1)}, bf16[48]{0:T(256)(128)(2,1)}, u32[]{:S(2)}) copy-start(bf16[48]{0:T(256)(128)(2,1)} %param.18) | copy-start | bytes 292
  7.3 9.7 %copy-start.175 = (bf16[48]{0:T(256)(128)(2,1)S(1)}, bf16[48]{0:T(256)(128)(2,1)}, u32[]{:S(2)}) copy-start(bf16[48]{0:T(256)(128)(2,1)} %param.19) | copy-start | bytes 292
  7.3 9.9 %copy-start.176 = (bf16[48]{0:T(256)(128)(2,1)S(1)}, bf16[48]{0:T(256)(128)(2,1)}, u32[]{:S(2)}) copy-start(bf16[48]{0:T(256)(128)(2,1)} %param.25) | copy-start | bytes 292
  7.3 10.1 %copy-start.177 = (bf16[192]{0:T(256)(128)(2,1)S(1)}, bf16[192]{0:T(256)(128)(2,1)}, u32[]{:S(2)}) copy-start(bf16[192]{0:T(256)(128)(2,1)} %param.28) | copy-start | bytes 1156
  7.3 92.0 %all-gather.5.cloned.1.call-start = ((), (), s32[]{:S(2)}) async-start(), calls=%async_computation.4 | async-start | bytes 3760128 | tf_op jit(solution)/shard_map/all_gather | solution.py:178
  8.0 136.0 %all-gather.7.cloned.1.call-start = ((), (), s32[]{:S(2)}) async-start(), calls=%async_computation.5 | async-start | bytes 1253376 | tf_op jit(solution)/shard_map/all_gather | solution.py:181
  8.8 216.8 %all-gather.9.cloned.1.call-start = ((), (), s32[]{:S(2)}) async-start(), calls=%async_computation.6 | async-start | bytes 5013504 | tf_op jit(solution)/shard_map/all_gather | solution.py:187
  9.5 297.9 %all-gather.11.cloned.1.call-start = ((), (), s32[]{:S(2)}) async-start(), calls=%async_computation.7 | async-start | bytes 5013504 | tf_op jit(solution)/shard_map/all_gather | solution.py:189
  10.1 511.1 %reduce-scatter.7.cloned.1.call-start = ((), (), s32[]{:S(2)}) async-start(), calls=%async_computation.9 | async-start | bytes 2433024 | tf_op jit(solution)/shard_map/reduce_scatter | solution.py:354
  14.9 88.2 %copy-start.106 = (f32[384]{0:T(512)}, f32[384]{0:T(512)S(1)}, u32[]{:S(2)}) copy-start(f32[384]{0:T(512)S(1)} %get-tuple-element.131) | copy-start | bytes 4612
  14.9 89.2 %copy-start.151 = (f32[384]{0:T(512)}, f32[384]{0:T(512)S(1)}, u32[]{:S(2)}) copy-start(f32[384]{0:T(512)S(1)} %get-tuple-element.132) | copy-start | bytes 4612
  15.5 88.7 %copy-start.156 = (f32[384]{0:T(512)}, f32[384]{0:T(512)S(1)}, u32[]{:S(2)}) copy-start(f32[384]{0:T(512)S(1)} %add_rsqrt_fusion.3) | copy-start | bytes 4612
  15.5 87.7 %copy-start.110 = (f32[384]{0:T(512)}, f32[384]{0:T(512)S(1)}, u32[]{:S(2)}) copy-start(f32[384]{0:T(512)S(1)} %add_rsqrt_fusion.1) | copy-start | bytes 4612
  99.3 15.4 %copy-start.87 = (pred[384,384]{0,1:T(8,128)(4,1)}, pred[384,384]{0,1:T(8,128)(4,1)S(1)}, u32[]{:S(2)}) copy-start(pred[384,384]{0,1:T(8,128)(4,1)S(1)} %get-tuple-element.134) | copy-start | bytes 442372
  108.1 9.0 %copy-start.30 = (bf16[384,768]{0,1:T(8,128)(2,1)}, bf16[384,768]{0,1:T(8,128)(2,1)S(1)}, u32[]{:S(2)}) copy-start(bf16[384,768]{0,1:T(8,128)(2,1)S(1)} %copy.137) | copy-start | bytes 1769476
  307.4 7.5 copy-start.166
  379.7 223.2 %reduce-scatter.5.cloned.1.call-start = ((), (), s32[]{:S(2)}) async-start(), calls=%async_computation.8 | async-start | bytes 7299072 | tf_op jit(solution)/shard_map/reduce_scatter | solution.py:351
  386.6 8.6 copy-start.56
  387.6 7.6 copy-start.57
  400.6 343.7 %reduce-scatter.11.cloned.1.call-start = ((), (), s32[]{:S(2)}) async-start(), calls=%async_computation.11 | async-start | bytes 9732096 | tf_op jit(solution)/shard_map/reduce_scatter | solution.py:360
  416.3 470.1 %reduce-scatter.9.cloned.1.call-start = ((), (), s32[]{:S(2)}) async-start(), calls=%async_computation.10 | async-start | bytes 9732096 | tf_op jit(solution)/shard_map/reduce_scatter | solution.py:358
  428.3 10.5 %copy-start.154 = (f32[768]{0:T(1024)S(1)}, f32[768]{0:T(1024)}, u32[]{:S(2)}) copy-start(f32[768]{0:T(1024)} %get-tuple-element.79) | copy-start | bytes 9220
  509.4 8.3 copy-start.165
  509.4 8.3 copy-start.164
  509.4 8.3 copy-start.62
  509.4 8.3 copy-start.63
  (157 other events, 440.0 us)
Sparse Core Ops, SparseCore 0:
  10.9 74.7 all-gather.4
  88.5 54.8 all-gather.6
  146.2 79.3 all-gather.8
  228.3 79.0 all-gather.10
  379.8 97.5 reduce-scatter.6
  484.5 118.3 reduce-scatter.4
  609.4 134.8 reduce-scatter.10
  751.8 134.5 reduce-scatter.8
where the time goes:
time: 899 us; the launch traced here: 893 us
  waiting for transfers between devices  513 us (57%)
  matrix products  151 us (17%)
  blocking collectives  121 us (13%)
  other arithmetic  45.9 us (5%)
  local copies, waits for them, and re-layouts  45.2 us (5%)
  between operations  17.6 us (2%)
    reduce_scatter x1, waiting for transfers between devices, per_device(): lax.psum_scatter(accum[9], ('fsdp', 'dp'), scatter_dimension=0, tiled=True)  142 us
    reduce_scatter x1, waiting for transfers between devices, per_device(): lax.psum_scatter(accum[11], ('fsdp', 'dp'), scatter_dimension=0, tiled=True)  141 us
    unnamed x2, blocking collectives  121 us
    reduce_scatter x1, waiting for transfers between devices, per_device(): lax.psum_scatter(accum[2], ('fsdp', 'dp'), scatter_dimension=0, tiled=True)  81.7 us
    all_gather x1, waiting for transfers between devices, per_device(): lax.all_gather(down_weight, 'fsdp', axis=0, tiled=True)  74.9 us
    all_gather x1, waiting for transfers between devices, per_device(): lax.all_gather(up_weight, 'fsdp', axis=0, tiled=True)  69.9 us
    dot_general x8, matrix products, product_left_turned(): lax.dot_general(left_side, right_side, (((0,), (0,)), ((), ())), preferre...  37.1 us
    dot_general x8, matrix products, product(): return jnp.dot(left_side, right_side, preferred_element_type=jnp.float32)  31.8 us
  transfers between devices with their start and end apart: 8, of which 5 were waited for; matrix products, arithmetic and copies ran while one was open for 18% of the time, Pallas kernels for 0%

commit v1 on v0

--- a/solution.py
+++ b/solution.py
@@ -1,8 +1,11 @@
+import functools
 import math
 
 import jax
 import jax.numpy as jnp
 from jax import lax
+from jax.experimental import pallas as pl
+from jax.experimental.pallas import tpu as pltpu
 from jax.sharding import PartitionSpec as P
 
 HEADS = 12
@@ -150,7 +153,7 @@
     )
 
 
-def per_device(
+def per_device_plain(
     tokens,
     segments,
     first_gain,
@@ -379,42 +382,631 @@
     )
 
 
+MESH = pl.DeviceIdType.MESH
+
+class Place:
+    def __init__(s, nz):
+        s.nz = nz
+        s.f = lax.axis_index("fsdp"); s.c = lax.axis_index("dp")
+        s.z = s.f // 4
+        s.p = s.f % 4
+        x = s.f % 2; y = (s.f // 2) % 2
+        a = jnp.where(s.c == 0, x, y); b = jnp.where(s.c == 0, y, x)
+        sa = jnp.where(s.c == 0, 1, 2); sb = jnp.where(s.c == 0, 2, 1)
+        s.pa = s.p + (1 - 2 * a) * sa
+        s.pb = s.p + (1 - 2 * b) * sb
+        s.pab = s.pa + (1 - 2 * b) * sb
+    def at(s, z, p, c=None):
+        return {"fsdp": z * 4 + p, "dp": s.c if c is None else c}
+
+def barrier(pc):
+    bar = pltpu.get_barrier_semaphore()
+    def sig(z, p, c=None):
+        pl.semaphore_signal(bar, inc=1, device_id=pc.at(z, p, c), device_id_type=MESH)
+    sig(pc.z, pc.pa); sig(pc.z, pc.pb); sig(pc.z, pc.p, 1 - pc.c)
+    for d in range(1, pc.nz):
+        @pl.when(pc.z >= d)
+        def _(): sig(pc.z - d, pc.p)
+        @pl.when(pc.z + d < pc.nz)
+        def _(): sig(pc.z + d, pc.p)
+    pl.semaphore_wait(bar, 3 + pc.nz - 1)
+
+def others(pc, fn):
+    for d in range(1, pc.nz):
+        @pl.when(pc.z + d < pc.nz)
+        def _(): fn(pc.z + d)
+        @pl.when(pc.z >= d)
+        def _(): fn(pc.z - d)
+
+class Gather:
+    def __init__(s, pc, k, kind, view, src, zs, ls, ss, so):
+        s.pc, s.k, s.kind, s.view, s.src = pc, k, kind, view, src
+        s.zs, s.ls, s.ss, s.so = zs, ls, ss, so
+    def rc(s, src, dst, ssem, rsem, dev):
+        return pltpu.make_async_remote_copy(src_ref=src, dst_ref=dst, send_sem=ssem, recv_sem=rsem, device_id=dev, device_id_type=MESH)
+    def zc(s, z2, zo=None):
+        pc = s.pc; v = s.view(pc.z if zo is None else zo, pc.p, pc.c)
+        return s.rc(s.src, v, s.ss.at[s.k, z2], s.zs.at[s.k, pc.z if zo is None else zo], pc.at(z2, pc.p))
+    def line(s, p, sem, dev, q):
+        pc = s.pc; v = s.view(None, p, pc.c)
+        return s.rc(v, v, s.so.at[s.k, q], s.ls.at[s.k, sem], dev)
+    def a1(s): return s.line(s.pc.p, 0, s.pc.at(s.pc.z, s.pc.pa), 0)
+    def b1(s): return s.line(s.pc.p, 1, s.pc.at(s.pc.z, s.pc.pb), 1)
+    def b2(s): return s.line(s.pc.pa, 2, s.pc.at(s.pc.z, s.pc.pb), 2)
+    def core(s, q):
+        pc = s.pc
+        return s.line((pc.p, pc.pa, pc.pb, pc.pab)[q], 3 + q, pc.at(pc.z, pc.p, 1 - pc.c), 3 + q)
+    def st0(s):
+        others(s.pc, lambda z2: s.zc(z2).start())
+    def st1(s):
+        pc = s.pc
+        others(pc, lambda z2: s.zc(z2, zo=z2).wait_recv())
+        s.a1().start(); s.b1().start(); s.core(0).start()
+    def st2(s):
+        s.a1().wait_recv()
+        s.b2().start(); s.core(1).start()
+    def st3(s):
+        s.b1().wait_recv(); s.core(2).start()
+    def st4(s):
+        s.b2().wait_recv(); s.core(3).start()
+    def fin(s):
+        for q in range(4): s.core(q).wait_recv()
+    def sent(s):
+        others(s.pc, lambda z2: s.zc(z2).wait_send())
+        s.a1().wait_send(); s.b1().wait_send(); s.b2().wait_send()
+        for q in range(4): s.core(q).wait_send()
+
+class GatherMinor(Gather):
+    def piece(s, p, sem, dev, q, src=None):
+        pc = s.pc; v = s.view(pc.z, p, pc.c)
+        return s.rc(v if src is None else src, v, s.so.at[s.k, q], s.ls.at[s.k, sem], dev)
+    def a1(s): return s.piece(s.pc.p, 0, s.pc.at(s.pc.z, s.pc.pa), 0, s.src)
+    def b1(s): return s.piece(s.pc.p, 1, s.pc.at(s.pc.z, s.pc.pb), 1, s.src)
+    def b2(s): return s.piece(s.pc.pa, 2, s.pc.at(s.pc.z, s.pc.pb), 2)
+    def zc(s, z2, zo=None):
+        pc = s.pc; v = s.view(pc.z if zo is None else zo, None, pc.c)
+        return s.rc(v, v, s.ss.at[s.k, z2], s.zs.at[s.k, pc.z if zo is None else zo], pc.at(z2, pc.p))
+    def corez(s, z):
+        pc = s.pc; v = s.view(z, None, pc.c)
+        return s.rc(v, v, s.so.at[s.k, 3 + z], s.ls.at[s.k, 3 + z], pc.at(pc.z, pc.p, 1 - pc.c))
+    def st0(s):
+        s.a1().start(); s.b1().start()
+    def st1(s):
+        s.a1().wait_recv(); s.b2().start()
+    def st2(s):
+        s.b1().wait_recv(); s.b2().wait_recv()
+        others(s.pc, lambda z2: s.zc(z2).start())
+        s.corez(s.pc.z).start()
+    def st3(s):
+        pass
+    def st4(s):
+        def go(z2):
+            s.zc(z2, zo=z2).wait_recv(); s.corez(z2).start()
+        others(s.pc, go)
+    def fin(s):
+        for z in range(s.pc.nz): s.corez(z).wait_recv()
+    def sent(s):
+        others(s.pc, lambda z2: s.zc(z2).wait_send())
+        s.a1().wait_send(); s.b1().wait_send(); s.b2().wait_send()
+        for z in range(s.pc.nz): s.corez(z).wait_send()
+BF=jnp.bfloat16; F32=jnp.float32
+EPS=EPSILON
+
+class GatherVec(Gather):
+    def a1(s): return s.line(s.pc.p, 0, s.pc.at(s.pc.z, s.pc.pa), 0)
+    def st1(s):
+        pc = s.pc
+        others(pc, lambda z2: s.zc(z2, zo=z2).wait_recv())
+        s.a1().start(); s.b1().start()
+    def st2(s):
+        s.a1().wait_recv(); s.b2().start()
+    def st3(s): s.b1().wait_recv()
+    def st4(s): s.b2().wait_recv()
+    def fin(s): pass
+    def sent(s):
+        others(s.pc, lambda z2: s.zc(z2).wait_send())
+        s.a1().wait_send(); s.b1().wait_send(); s.b2().wait_send()
+
+class GatherMinorR(GatherMinor):
+    def up(s, zo):
+        pc=s.pc; v=s.view(zo,None,pc.c)
+        return s.rc(v,v,s.ss.at[s.k,zo],s.zs.at[s.k,zo],pc.at(pc.z+1,pc.p))
+    def dn(s, zo):
+        pc=s.pc; v=s.view(zo,None,pc.c)
+        return s.rc(v,v,s.so.at[s.k,7+zo],s.zs.at[s.k,zo],pc.at(pc.z-1,pc.p))
+    def st2(s):
+        pc=s.pc
+        s.b1().wait_recv(); s.b2().wait_recv()
+        @pl.when(pc.z<pc.nz-1)
+        def _(): s.up(pc.z).start()
+        @pl.when(pc.z>0)
+        def _(): s.dn(pc.z).start()
+        s.corez(pc.z).start()
+    def relay(s,d):
+        pc=s.pc
+        @pl.when(pc.z>=d)
+        def _():
+            s.up(pc.z-d).wait_recv()
+            @pl.when(pc.z<pc.nz-1)
+            def _(): s.up(pc.z-d).start()
+            s.corez(pc.z-d).start()
+        @pl.when(pc.z+d<pc.nz)
+        def _():
+            s.up(pc.z+d).wait_recv()
+            @pl.when(pc.z>0)
+            def _(): s.dn(pc.z+d).start()
+            s.corez(pc.z+d).start()
+    def st3(s): s.relay(1)
+    def st4(s):
+        for d in range(2,s.pc.nz): s.relay(d)
+    def sent(s):
+        pc=s.pc
+        for d in range(pc.nz):
+            @pl.when((pc.z>=d)&(pc.z<pc.nz-1))
+            def _(): s.up(pc.z-d).wait_send()
+            @pl.when((pc.z+d<pc.nz)&(pc.z>0))
+            def _(): s.dn(pc.z+d).wait_send()
+        s.a1().wait_send(); s.b1().wait_send(); s.b2().wait_send()
+        for z in range(s.pc.nz): s.corez(z).wait_send()
+
+def dotT(a,b): return lax.dot_general(a,b,(((1,),(1,)),((),())),preferred_element_type=F32)
+def dot(a,b): return jnp.dot(a,b,preferred_element_type=F32)
+def dotL(a,b): return lax.dot_general(a,b,(((0,),(0,)),((),())),preferred_element_type=F32)
+
+def loop(n, body, events=()):
+    ev={}
+    for i,fn in events: ev.setdefault(min(i,n-1),[]).append(fn)
+    def step(i,_):
+        body(i)
+        for j in sorted(ev):
+            @pl.when(i==j)
+            def _():
+                for fn in ev[j]: fn()
+        return 0
+    lax.fori_loop(0,n,step,0)
+
+def norm(x, g, b):
+    mean=jnp.mean(x,axis=-1,keepdims=True)
+    cen=x-mean
+    inv=lax.rsqrt(jnp.mean(cen*cen,axis=-1,keepdims=True)+EPS)
+    return (cen*inv)*g+b
+
+def chunks(D, FF, down_rows):
+    h=down_rows//2
+    return [(0,0,None,0,D,'M'),(0,0,None,2*D,D//2,'M'),(1,0,None,0,D//2,'M'),(2,0,None,0,FF//4,'M'),(2,0,None,FF//2,FF//4,'M'),(3,0,h,0,D//2,'M'),(3,h,h,0,D//2,'N')]
+
+def k1_body(D,FF,H,NZ,nseq,S,ev_lag, *refs):
+    (tok,segr,slab,wq,wo,wu,wd,
+     out_h,qkv_h,pt_h,att_h,hid_h,n1_h,n2_h,act_h,slp_h,gq_h,go_h,gu_h,gd_h,vec_h,
+     gq,go,gu,gd,vbuf,n1,qkv,att,hid,n2,act,slp,outb,pst,bias,vec,upb,n1t,n2t,attt,actt,
+     zs,lsem,ss,so,loc,hsem,psem)=refs
+    R=nseq*S
+    pc=Place(NZ)
+    bufs=[gq,go,gu,gd]; ws=[wq,wo,wu,wd]
+    CH=chunks(D,FF,wd.shape[0])
+    gs=[]; own=[]
+    for k,(wi,r0,nr,c0,ncol,kind) in enumerate(CH):
+        nr=ws[wi].shape[0] if nr is None else nr
+        def view(z,p,c,wi=wi,r0=r0,nr=nr,c0=c0,ncol=ncol):
+            zi=slice(None) if z is None else z
+            pi=slice(None) if p is None else p
+            return bufs[wi].at[zi,pi,pl.ds(r0,nr),pl.ds(pl.multiple_of(c*ncol+c0,128),ncol)]
+        src=ws[wi].at[pl.ds(r0,nr),pl.ds(pl.multiple_of(pc.c*ncol+c0,128),ncol)]
+        gs.append((Gather if kind=='M' else GatherMinorR)(pc,k,kind,view,src,zs,lsem,ss,so))
+        cp=pltpu.make_async_copy(src, view(pc.z,pc.p,pc.c), loc.at[k]); cp.start(); own.append(cp)
+    def vview(z,p,c):
+        return vbuf.at[slice(None) if z is None else z, slice(None) if p is None else p]
+    kv=len(CH)
+    gv=GatherVec(pc,kv,'V',vview,slab,zs,lsem,ss,so)
+    cp=pltpu.make_async_copy(slab, vview(pc.z,pc.p,pc.c), loc.at[kv]); cp.start(); own.append(cp)
+    barrier(pc)
+    gv.st0(); gs[0].st0()
+    gs[6].st0()
+    for k in range(1,6): gs[k].st0()
+    for cp in own: cp.wait()
+    sends=[]
+    def put(src,dst,sem):
+        c=pltpu.make_async_copy(src,dst,sem); c.start(); sends.append(c)
+    for q in range(nseq):
+        row=jnp.broadcast_to(segr[q:q+1,:],(S,S))
+        bias[q]=jnp.where(row==row.T,0.0,-1e30).astype(F32)
+    gv.st1(); gs[0].st1(); gs[6].st1(); gs[1].st1()
+    gv.st2(); gv.st3(); gs[0].st2(); gs[0].st3(); gv.st4()
+    rows=[vbuf[i//4,i%4] for i in range(4*NZ)]
+    nv=D//(4*NZ)
+    vec[...]=jnp.concatenate([r[:,:nv] for r in rows],axis=1)
+    upb[...]=jnp.concatenate([jnp.concatenate([r[8:9,:],r[9:10,:FF//(4*NZ)-128]],axis=1) for r in rows],axis=1)
+    gs[6].st2(); gs[1].st2(); gs[2].st1()
+    BR=128
+    def n1b(i):
+        r=pl.ds(pl.multiple_of(i*BR,BR),BR)
+        y=norm(tok[r,:].astype(F32),vec[0:1,:],vec[1:2,:]).astype(BF)
+        n1[r,:]=y
+        n1t[:,r]=y.T
+    loop(R//BR,n1b)
+    gs[0].st4(); gs[1].st3(); gs[3].st1(); gs[2].st2()
+    put(n1t,n1_h,hsem.at[0]); put(vec,vec_h,hsem.at[1])
+    gs[0].fin()
+    TN=256
+    def qk(j):
+        c=pl.ds(pl.multiple_of(j*TN,TN),TN)
+        w=gq[:,:,:,c].reshape(D,TN)
+        y=dot(n1[...],w)
+        nq=D//TN
+        cb=pl.ds(pl.multiple_of((j%nq)*TN,TN),TN)
+        b=jnp.where(j<nq,vec[2:3,cb],jnp.where(j<2*nq,0.0,vec[3:4,cb]))
+        qkv[pl.ds(pl.multiple_of((j//nq)*R,128),R),cb]=(y+b).astype(BF)
+    loop(2*D//TN,qk)
+    gs[1].st4(); gs[2].st3(); gs[3].st2(); gs[4].st1()
+    gs[1].fin()
+    loop(D//TN,lambda j: qk(j+2*D//TN))
+    put(qkv,qkv_h,hsem.at[3])
+    put(gq,gq_h,hsem.at[4])
+    gs[2].st4()
+    HP=H//2
+    lane=lax.broadcasted_iota(jnp.int32,(1,128),1)
+    def attn(i):
+        s=i//HP; hp=i%HP
+        r=pl.ds(pl.multiple_of(s*S,128),S)
+        hc=pl.ds(pl.multiple_of(hp*128,128),128)
+        q2,k2,v2=[qkv[pl.ds(pl.multiple_of(w*R+s*S,128),S),hc] for w in range(3)]
+        vT=v2.T
+        sl=i%2
+        @pl.when(i>=2)
+        def _(): pltpu.make_async_copy(pst.at[sl],pt_h.at[i-2],psem.at[sl]).wait()
+        os_=[]
+        for h in range(2):
+            qm=jnp.where((lane>=64) if h else (lane<64),q2*BF(0.125),BF(0))
+            sT=dotT(k2,qm)+bias[s]
+            m=jnp.max(sT,axis=0,keepdims=True)
+            e=jnp.exp(sT-m)
+            l=jnp.sum(e,axis=0,keepdims=True)
+            p=(e*(1.0/l)).astype(BF)
+            pst[sl,h]=p
+            os_.append(dot(vT[64*h:64*h+64],p))
+        oT=jnp.concatenate(os_,axis=0).astype(BF)
+        attt[hc,r]=oT
+        att[r,hc]=oT.T
+        pltpu.make_async_copy(pst.at[sl],pt_h.at[i],psem.at[sl]).start()
+    loop(2*HP if nseq==2 else nseq*HP,attn,[(0,gs[3].st3),(1,gs[4].st2),(2,gs[5].st1),(4,gs[3].st4),(5,gs[6].st3),(6,gs[4].st3),(8,gs[5].st2),(9,gs[4].st4)])
+    put(attt,att_h,hsem.at[5])
+    gs[2].fin()
+    put(go,go_h,hsem.at[6])
+    def op(j):
+        c=pl.ds(pl.multiple_of(j*TN,TN),TN)
+        w=go[:,:,:,c].reshape(D,TN)
+        hid[:,c]=dot(att[...],w)+vec[4:5,c]+tok[:,c].astype(F32)
+    loop(D//TN,op)
+    put(hid,hid_h,hsem.at[7])
+    gs[5].st3()
+    def n2b(i):
+        r=pl.ds(pl.multiple_of(i*BR,BR),BR)
+        y=norm(hid[r,:],vec[5:6,:],vec[6:7,:]).astype(BF)
+        n2[r,:]=y
+        n2t[:,r]=y.T
+    loop(R//BR,n2b)
+    put(n2t,n2_h,hsem.at[8])
+    gs[3].fin()
+    def upj(j):
+        c=pl.ds(pl.multiple_of(j*TN,TN),TN)
+        w=gu[:,:,:,c].reshape(D,TN)
+        u=dot(n2[...],w)+upb[:,c]
+        u2=u*u
+        t=jnp.tanh(SLOPE*(u+CUBIC*u*u2))
+        hp1=0.5*(1.0+t)
+        a=(u*hp1).astype(BF)
+        act[:,c]=a
+        actt[c,:]=a.T
+        slp[:,c]=(hp1+0.5*u*(1.0-t*t)*(SLOPE*(1.0+3.0*CUBIC*u2))).astype(BF)
+    loop(FF//2//TN,upj,[(2,gs[5].st4)])
+    gs[4].fin()
+    put(gu,gu_h,hsem.at[9])
+    loop(FF//2//TN,lambda j: upj(j+FF//2//TN),[(2,gs[6].st4)])
+    put(actt,act_h,hsem.at[10]); put(slp,slp_h,hsem.at[11])
+    gs[5].fin(); gs[6].fin()
+    put(gd,gd_h,hsem.at[12])
+    def dn(j):
+        c=pl.ds(pl.multiple_of(j*TN,TN),TN)
+        w=gd[:,:,:,c].reshape(FF,TN)
+        outb[:,c]=(dot(act[...],w)+vec[7:8,c]+hid[:,c]).astype(BF)
+    loop(D//TN,dn)
+    put(outb,out_h,hsem.at[13])
+    n=nseq*HP
+    for i in (n-2,n-1):
+        pltpu.make_async_copy(pst.at[i%2],pt_h.at[i],psem.at[i%2]).wait()
+    for g in gs: g.sent()
+    gv.sent()
+    for c in sends: c.wait()
+
+def k1_call(tok,segr,slab,wq,wo,wu,wd,D,FF,H,NZ):
+    nseq,S=tok.shape[0],tok.shape[1]
+    R=nseq*S
+    sds=jax.ShapeDtypeStruct
+    g4=[(NZ,4)+w.shape for w in (wq,wo,wu,wd)]
+    outs=[sds((R,D),BF),sds((3*R,D),BF),sds((nseq*H//2,2,S,S),BF),sds((D,R),BF),sds((R,D),F32),sds((D,R),BF),sds((D,R),BF),sds((FF,R),BF),sds((R,FF),BF)]+[sds(g,BF) for g in g4]+[sds((16,D),F32)]
+    V=pltpu.VMEM
+    n=8
+    scr=[V(g,BF) for g in g4]+[V((NZ,4,16,128),F32),V((R,D),BF),V((3*R,D),BF),V((R,D),BF),V((R,D),F32),V((R,D),BF),V((R,FF),BF),V((R,FF),BF),V((R,D),BF),V((2,2,S,S),BF),V((nseq,S,S),F32),V((16,D),F32),V((1,FF),F32),V((D,R),BF),V((D,R),BF),V((D,R),BF),V((FF,R),BF)]
+    dma=pltpu.SemaphoreType.DMA
+    scr+=[dma((n,NZ)),dma((n,7)),dma((n,NZ)),dma((n,7+NZ)),dma((n,)),dma((14,)),dma((2,))]
+    vm=pl.BlockSpec(memory_space=pltpu.VMEM); anyb=pl.BlockSpec(memory_space=pl.ANY)
+    flops=2*R*D*(4*D+2*FF)
+    return pl.pallas_call(functools.partial(k1_body,D,FF,H,NZ,nseq,S,1),
+        out_shape=outs,in_specs=[vm]*7,out_specs=[anyb]*len(outs),scratch_shapes=scr,name="gather_forward",
+        compiler_params=pltpu.CompilerParams(collective_id=0,has_side_effects=True,vmem_limit_bytes=63*1024*1024))(
+        tok.reshape(R,D),segr,slab,wq,wo,wu,wd)
+
+def make_slab(vs, upb):
+    m=vs[0].shape[0]; L=upb.shape[0]
+    rows=[jnp.pad(v.astype(F32)[None],((0,0),(0,128-m))) for v in vs]
+    u=upb.astype(F32)
+    rows.append(u[None,:128]); rows.append(jnp.pad(u[None,128:],((0,0),(0,256-L))))
+    return jnp.pad(jnp.concatenate(rows,axis=0),((0,6),(0,0)))
+
+class Scatter:
+    def __init__(s, pc, k, g, pb_, bb, ab, zb, out, sem, zsem, kv):
+        s.pc,s.k,s.g,s.pb_,s.bb,s.ab,s.zb,s.out,s.sem,s.zsem=pc,k,g,pb_,bb,ab,zb,out,sem,zsem
+    def rc(s,src,dst,q,dev):
+        return pltpu.make_async_remote_copy(src_ref=src,dst_ref=dst,send_sem=s.sem.at[s.k,0,q],recv_sem=s.sem.at[s.k,1,q],device_id=dev,device_id_type=MESH)
+    def pair(s):
+        pc=s.pc
+        return s.rc(s.g.at[1-pc.c], s.pb_, 0, pc.at(pc.z,pc.p,1-pc.c))
+    def b(s,w):
+        pc=s.pc
+        return s.rc(s.g.at[pc.c,:,(pc.pb,pc.pab)[w]], s.bb.at[w], 1+w, pc.at(pc.z,pc.pb))
+    def a(s):
+        pc=s.pc
+        return s.rc(s.g.at[pc.c,:,pc.pa], s.ab, 3, pc.at(pc.z,pc.pa))
+    def zc(s,z2):
+        pc=s.pc
+        return pltpu.make_async_remote_copy(src_ref=s.g.at[pc.c,z2,pc.p],dst_ref=s.zb.at[pc.z],send_sem=s.zsem.at[s.k,0,z2],recv_sem=s.zsem.at[s.k,1,pc.z],device_id=pc.at(z2,pc.p),device_id_type=MESH)
+    def zr(s,zo):
+        pc=s.pc
+        return pltpu.make_async_remote_copy(src_ref=s.g.at[pc.c,zo,pc.p],dst_ref=s.zb.at[zo],send_sem=s.zsem.at[s.k,0,zo],recv_sem=s.zsem.at[s.k,1,zo],device_id=pc.at(zo,pc.p),device_id_type=MESH)
+    def stP(s): s.pair().start()
+    def stB(s):
+        pc=s.pc; s.pair().wait_recv()
+        for w,p in enumerate((pc.pb,pc.pab)):
+            def add(z,_,p=p):
+                s.g[pc.c,z,p]=s.g[pc.c,z,p]+s.pb_[z,p]
+                return 0
+            lax.fori_loop(0,pc.nz,add,0)
+        s.b(0).start(); s.b(1).start()
+    def stA(s):
+        pc=s.pc; s.b(1).wait_recv()
+        def add(z,_):
+            s.g[pc.c,z,pc.pa]=(s.g[pc.c,z,pc.pa].astype(F32)+s.pb_[z,pc.pa].astype(F32)+s.bb[1,z].astype(F32)).astype(s.g.dtype)
+            return 0
+        lax.fori_loop(0,pc.nz,add,0)
+        s.a().start()
+    def stZ(s):
+        pc=s.pc; s.b(0).wait_recv(); s.a().wait_recv()
+        def add(z,_):
+            s.g[pc.c,z,pc.p]=(s.g[pc.c,z,pc.p].astype(F32)+s.pb_[z,pc.p].astype(F32)+(s.bb[0,z].astype(F32)+s.ab[z].astype(F32))).astype(s.g.dtype)
+            return 0
+        lax.fori_loop(0,pc.nz,add,0)
+        others(pc, lambda z2: s.zc(z2).start())
+    def stF(s):
+        pc=s.pc
+        others(pc, lambda z2: s.zr(z2).wait_recv())
+        s.zb[pc.z]=s.g[pc.c,pc.z,pc.p]
+        t=s.zb[0].astype(F32)
+        for z in range(1,pc.nz): t=t+s.zb[z].astype(F32)
+        s.out(t)
+    def sent(s):
+        s.pair().wait_send(); s.b(0).wait_send(); s.b(1).wait_send(); s.a().wait_send()
+        others(s.pc, lambda z2: s.zc(z2).wait_send())
+
+def k2_body(D,FF,H,NZ,nseq,S,*refs):
+    (actT_h,cot_h,gd_h,slp_h,n2T_h,gu_h,hid_h,attT_h,go_h,qkv_h,pt_h,gq_h,n1T_h,tok_h,vec_h,
+     tg_h,o_q,o_o,o_u,o_d,*rest)=refs
+    o_v=rest[:9]
+    (actT,cot,gd,slp,n2T,gu,hid,attT,go,vec,pst,dn,br,datt,dqkv,vg,ug,
+     gd0,gd1,*rest)=rest[9:]
+    (p0,p1,p2,p3,p4,p5,p6,b0,b1,b2,b3,b4,b5,b6,a0,a1,a2,a3,a4,a5,a6,z0,z1,z2,z3,z4,z5,z6,
+     gu0,gu1,gout,gv,vgb,vp,vb,va,vz,sem,zsem,lsem,psem,osem)=rest
+    R=nseq*S
+    pc=Place(NZ)
+    qkv,n1T,gq,tok,gqk=actT.at[pl.ds(0,3*R)],actT.at[pl.ds(3*R,R)],gd,n2T,gd0
+    names=[actT,cot,gd,slp,n2T,gu,hid,attT,go,qkv,None,n1T,tok,vec]
+    srcs=[actT_h,cot_h,gd_h,slp_h,n2T_h,gu_h,hid_h,attT_h,go_h,qkv_h,None,n1T_h,tok_h,vec_h]
+    ld={}
+    def fetch(*ks):
+        for i in ks:
+            ld[i]=pltpu.make_async_copy(srcs[i],names[i],lsem.at[i]); ld[i].start()
+    need=lambda *ks: [ld[k].wait() for k in ks]
+    gqc=[pltpu.make_async_copy(gq_h.at[:,pl.ds(w*D,D)],gq.at[pl.ds(w*D,D)],lsem.at[14+w]) for w in range(3)]
+    fetch(0,1,2,3,4,5,6,13,7,8)
+    barrier(pc)
+    rr=D//(8*NZ); rd=FF//(8*NZ)
+    def outd(r0):
+        def fn(t):
+            for w in range(2): o_d[pl.ds(r0+w*rr,rr),:]=t[:,w*D:(w+1)*D]
+        return fn
+    def outw(ref,r0,c0):
+        def fn(t):
+            ref[pl.ds(r0,t.shape[0]),pl.ds(c0,t.shape[1])]=t
+        return fn
+    HF=FF//2
+    sc=[Scatter(pc,0,gd0,p0,b0,a0,z0,outd(0),sem,zsem,0),
+        Scatter(pc,1,gd1,p1,b1,a1,z1,outd(rd//2),sem,zsem,0),
+        Scatter(pc,2,gu0,p2,b2,a2,z2,outw(o_u,0,0),sem,zsem,0),
+        Scatter(pc,3,gu1,p3,b3,a3,z3,outw(o_u,0,HF),sem,zsem,0),
+        Scatter(pc,4,gout,p4,b4,a4,z4,outw(o_o,0,0),sem,zsem,0),
+        Scatter(pc,5,gqk,p5,b5,a5,z5,outw(o_q,0,0),sem,zsem,0),
+        Scatter(pc,6,gv,p6,b6,a6,z6,outw(o_q,0,2*D),sem,zsem,0)]
+    TN=256
+    lanes=lambda j,w=TN: pl.ds(pl.multiple_of(j*w,128),w)
+    vg[...]=jnp.zeros_like(vg)
+    need(0,1)
+    def l1(i):
+        y=dot(actT[pl.ds(pl.multiple_of(i*4*rd,128),4*rd),:],cot[...]).astype(BF)
+        for d in range(2):
+            for c in range(2):
+                for h,g in enumerate((gd0,gd1)):
+                    o=(d*2+c)*rd+h*(rd//2)
+                    for w in range(2): g[c,i//2,2*(i%2)+d,:,w*D:(w+1)*D]=y[o+w*rr:o+(w+1)*rr]
+    loop(2*NZ,l1)
+    sc[0].stP(); sc[1].stP()
+    fetch(9,11)
+    need(2,3)
+    def l2(j):
+        c=lanes(j)
+        da=dotT(cot[...],gd[pl.ds(pl.multiple_of(j*TN,TN),TN),:])
+        du=(da*slp[:,c].astype(F32)).astype(BF)
+        slp[:,c]=du
+        ug[:,c]=jnp.sum(du.astype(F32),axis=0,keepdims=True)
+    loop(FF//TN,l2,[(3,sc[0].stB),(6,sc[1].stB)])
+    for c in gqc: c.start()
+    need(4)
+    def scat(g,lhs,rhs,rhs_c,g_c):
+        y=dot(lhs[...],rhs[:,rhs_c]).reshape(NZ,4,2,rr,TN)
+        for c in range(2):
+            for z in range(NZ):
+                g[c,z,:,:,g_c]=y[z,:,c].astype(BF)
+    nh=HF//TN
+    loop(nh,lambda j: scat(gu0,n2T,slp,lanes(j),lanes(j)),[(2,sc[0].stA)])
+    sc[2].stP()
+    loop(nh,lambda j: scat(gu1,n2T,slp,lanes(j+nh),lanes(j)),[(2,sc[1].stA),(3,sc[2].stB)])
+    sc[3].stP()
+    fetch(12)
+    need(5)
+    def l4(j):
+        dn[:,lanes(j)]=dotT(slp[...],gu[pl.ds(pl.multiple_of(j*TN,TN),TN),:])
+    loop(D//TN,l4,[(0,sc[0].stZ),(1,sc[3].stB)])
+    need(6,13)
+    BR=128
+    def back(x,g,gain,top):
+        mean=jnp.mean(x,axis=-1,keepdims=True)
+        cen=x-mean
+        inv=lax.rsqrt(jnp.mean(cen*cen,axis=-1,keepdims=True)+EPS)
+        unit=cen*inv
+        sg=g*gain
+        inner=sg-jnp.mean(sg,axis=-1,keepdims=True)-unit*jnp.mean(sg*unit,axis=-1,keepdims=True)
+        return top+inner*inv, jnp.sum(g*unit,axis=0,keepdims=True), jnp.sum(g,axis=0,keepdims=True)
+    def l5(i):
+        r=pl.ds(pl.multiple_of(i*BR,BR),BR)
+        ct=cot[r,:].astype(F32)
+        h,gg,gs=back(hid[r,:],dn[r,:],vec[5:6,:],ct)
+        hid[r,:]=h
+        hb=h.astype(BF)
+        br[r,:]=hb
+        vg[5:6,:]+=gg; vg[6:7,:]+=gs
+        vg[4:5,:]+=jnp.sum(hb.astype(F32),axis=0,keepdims=True)
+        vg[7:8,:]+=jnp.sum(ct,axis=0,keepdims=True)
+    loop(R//BR,l5,[(2,sc[1].stZ),(4,sc[2].stA)])
+    need(7,8)
+    loop(D//TN,lambda j: scat(gout,attT,br,lanes(j),lanes(j)),[(1,sc[0].stF)])
+    sc[4].stP()
+    def l6(j):
+        datt[:,lanes(j)]=dotT(br[...],go[pl.ds(pl.multiple_of(j*TN,TN),TN),:]).astype(BF)
+    loop(D//TN,l6,[(0,sc[3].stA),(1,sc[4].stB)])
+    need(9)
+    HP=H//2
+    n=nseq*HP
+    lane=lax.broadcasted_iota(jnp.int32,(1,128),1)
+    pcopy=lambda i: pltpu.make_async_copy(pt_h.at[i],pst.at[i%2],psem.at[i%2])
+    pcopy(0).start()
+    def l7(i):
+        s=i//HP; hp=i%HP
+        r=pl.ds(pl.multiple_of(s*S,128),S)
+        c0,c1,c2=[pl.ds(pl.multiple_of(w*D+hp*128,128),128) for w in range(3)]
+        pcopy(i).wait()
+        @pl.when(i+1<n)
+        def _(): pcopy(i+1).start()
+        q2,k2,v2=[actT[pl.ds(pl.multiple_of(w*R+s*S,128),S),c0] for w in range(3)]; da=datt[r,c0]
+        kT=k2.T
+        dq=[];dk=[];dv=[]
+        for h in range(2):
+            lo=(lane>=64) if h else (lane<64)
+            pT=pst[i%2,h]
+            dv.append(dot(pT,da))
+            dpT=dotT(v2,jnp.where(lo,da,BF(0)))
+            pf=pT.astype(F32)
+            t=dpT*pf
+            ds=(t-pf*jnp.sum(t,axis=0,keepdims=True)).astype(BF)
+            dk.append(dot(ds,q2))
+            dq.append(dot(kT[64*h:64*h+64],ds))
+        dvv=jnp.where(lane<64,dv[0],dv[1]).astype(BF)
+        dkk=(jnp.where(lane<64,dk[0],dk[1])*0.125).astype(BF)
+        dqq=(jnp.concatenate(dq,axis=0).T*0.125).astype(BF)
+        dqkv[r,c0]=dqq; dqkv[r,c1]=dkk; dqkv[r,c2]=dvv
+        vg[2:3,c0]+=jnp.sum(dqq.astype(F32),axis=0,keepdims=True)
+        vg[3:4,c0]+=jnp.sum(dvv.astype(F32),axis=0,keepdims=True)
+    loop(n,l7,[(1,sc[2].stZ),(2,sc[1].stF),(3,sc[4].stA),(5,sc[3].stZ),(6,sc[2].stF),(8,sc[4].stZ),(10,sc[3].stF),(11,sc[4].stF)])
+    need(11)
+    sc[0].sent()
+    nq=D//TN
+    loop(2*nq,lambda j: scat(gqk,n1T,dqkv,lanes(j),lanes(j)))
+    sc[5].stP()
+    loop(nq,lambda j: scat(gv,n1T,dqkv,lanes(j+2*nq),lanes(j)),[(0,sc[5].stB)])
+    sc[6].stP()
+    for c in gqc: c.wait()
+    need(12)
+    def l9(j):
+        dn[:,lanes(j)]=sum(dotT(dqkv[:,w*D:(w+1)*D],gq[pl.ds(pl.multiple_of(w*D+j*TN,TN),TN),:]) for w in range(3))
+    loop(nq,l9,[(0,sc[6].stB)])
+    def l10(i):
+        r=pl.ds(pl.multiple_of(i*BR,BR),BR)
+        t,gg,gs=back(tok[r,:].astype(F32),dn[r,:],vec[0:1,:],hid[r,:])
+        dn[r,:]=t
+        vg[0:1,:]+=gg; vg[1:2,:]+=gs
+    loop(R//BR,l10,[(2,sc[5].stA)])
+    oc=pltpu.make_async_copy(dn,tg_h,osem.at[0]); oc.start()
+    nv=D//(4*NZ); nu=FF//(4*NZ)
+    for i in range(4*NZ):
+        for c in range(2):
+            vgb[c,i//4,i%4]=jnp.concatenate([jnp.pad(vg[0:8,nv*i+c*(nv//2):nv*i+(c+1)*(nv//2)],((0,0),(0,128-nv//2))),
+               jnp.pad(ug[:,nu*i+c*(nu//2):nu*i+(c+1)*(nu//2)],((0,7),(0,128-nu//2)))],axis=0)
+    def outv(t):
+        for q in range(8): o_v[q][...]=t[q:q+1,:nv//2]
+        o_v[8][...]=t[8:9,:nu//2]
+    sv=Scatter(pc,7,vgb,vp,vb,va,vz,outv,sem,zsem,0)
+    sv.stP()
+    sc[6].stA();
+    sv.stB(); sc[5].stZ(); sc[6].stZ(); sv.stA(); sv.stZ()
+    sc[5].stF(); sc[6].stF(); sv.stF()
+    for s in sc[1:]+[sv]: s.sent()
+    oc.wait()
+
+def k2_call(sv,cot,tok,D,FF,H,NZ,S):
+    (qkv,pt,attT,hid,n1T,n2T,actT,slp,gq,go,gu,gd,vec)=sv
+    R=n1T.shape[1]; nseq=R//S
+    sds=jax.ShapeDtypeStruct; V=pltpu.VMEM; dma=pltpu.SemaphoreType.DMA
+    rr=D//(8*NZ); rd=FF//(8*NZ); nd=8*NZ
+    ins=(actT,cot.reshape(R,D),gd.reshape(FF,D),slp,n2T,gu.reshape(D,FF),hid,attT,go.reshape(D,D),qkv,pt,gq.reshape(D,3*D),n1T,tok.reshape(R,D),vec)
+    outs=[sds((R,D),F32),sds((rr,3*D),F32),sds((rr,D),F32),sds((rr,FF),F32),sds((rd,D),F32)]+[sds((1,rr),F32)]*8+[sds((1,rd),F32)]
+    vm=pl.BlockSpec(memory_space=pltpu.VMEM); anyb=pl.BlockSpec(memory_space=pl.ANY)
+    pieces=[(rr,FF//2),(rr,FF//2),(rr,FF//2),(rr,FF//2),(rr,D),(rr,2*D),(rr,D)]
+    scr=[V((FF,R),BF),V((R,D),BF),V((FF,D),BF),V((R,FF),BF),V((D,R),BF),V((D,FF),BF),V((R,D),F32),V((D,R),BF),V((D,D),BF),V((16,D),F32),
+        V((2,2,S,S),BF),V((R,D),F32),V((R,D),BF),V((R,D),BF),V((R,3*D),BF),V((16,D),F32),V((1,FF),F32)]
+    scr+=[V((2,NZ,4)+p,BF) for p in pieces[:2]]
+    scr+=[V((NZ,4)+p,BF) for p in pieces]+[V((2,NZ)+p,BF) for p in pieces]+[V((NZ,)+p,BF) for p in pieces]+[V((NZ,)+p,BF) for p in pieces]
+    scr+=[V((2,NZ,4)+p,BF) for p in (pieces[2],pieces[3],pieces[4],pieces[6])]
+    vp=(16,128)
+    scr+=[V((2,NZ,4)+vp,F32),V((NZ,4)+vp,F32),V((2,NZ)+vp,F32),V((NZ,)+vp,F32),V((NZ,)+vp,F32)]
+    scr+=[dma((8,2,4)),dma((8,2,NZ)),dma((17,)),dma((2,)),dma((1,))]
+    o=pl.pallas_call(functools.partial(k2_body,D,FF,H,NZ,nseq,S),out_shape=outs,in_specs=[anyb]*15,
+        out_specs=[anyb]+[vm]*(len(outs)-1),scratch_shapes=scr,name="backward_scatter",
+        compiler_params=pltpu.CompilerParams(collective_id=1,has_side_effects=True,vmem_limit_bytes=67043328))(*ins)
+    return o
+def per_device(NZ,tokens,segments,first_gain,first_shift,qkv_weight,query_bias,value_bias,out_weight,out_bias,second_gain,second_shift,up_weight,up_bias,down_weight,down_bias,cotangent):
+    D=tokens.shape[2]; FF=up_weight.shape[1]; S=tokens.shape[1]; H=HEADS
+    slab=make_slab((first_gain,first_shift,query_bias,value_bias,out_bias,second_gain,second_shift,down_bias),up_bias)
+    out,*sv=k1_call(tokens,segments,slab,qkv_weight,out_weight,up_weight,down_weight,D,FF,H,NZ)
+    tg,oq,oo,ou,od,*v=k2_call(sv,cotangent,tokens,D,FF,H,NZ,S)
+    v=[a.reshape(-1) for a in v]
+    return (out.reshape(tokens.shape),tg.reshape(tokens.shape),v[0],v[1],oq,v[2],v[3],oo,v[4],v[5],v[6],ou,v[8],od,v[7])
+def specs_of(start):
+    pass
 def solution(mesh):
-    in_specs = (
-        P(("fsdp", "dp"), None, None),
-        P(("fsdp", "dp"), None),
-        P("fsdp"),
-        P("fsdp"),
-        P("fsdp", None),
-        P("fsdp"),
-        P("fsdp"),
-        P("fsdp", None),
-        P("fsdp"),
-        P("fsdp"),
-        P("fsdp"),
-        P("fsdp", None),
-        P("fsdp"),
-        P("fsdp", None),
-        P("fsdp"),
-        P(("fsdp", "dp"), None, None),
-    )
-    out_specs = (
-        P(("fsdp", "dp"), None, None),
-        P(("fsdp", "dp"), None, None),
-        P(("fsdp", "dp")),
-        P(("fsdp", "dp")),
-        P(("fsdp", "dp"), None),
-        P(("fsdp", "dp")),
-        P(("fsdp", "dp")),
-        P(("fsdp", "dp"), None),
-        P(("fsdp", "dp")),
-        P(("fsdp", "dp")),
-        P(("fsdp", "dp")),
-        P(("fsdp", "dp"), None),
-        P(("fsdp", "dp")),
-        P(("fsdp", "dp"), None),
-        P(("fsdp", "dp")),
-    )
-    return jax.shard_map(
-        per_device, mesh=mesh, in_specs=in_specs, out_specs=out_specs, check_vma=False
-    )
+    d=("fsdp","dp")
+    ins=(P(d,None,None),P(d,None),P("fsdp"),P("fsdp"),P("fsdp",None),P("fsdp"),P("fsdp"),P("fsdp",None),P("fsdp"),P("fsdp"),P("fsdp"),P("fsdp",None),P("fsdp"),P("fsdp",None),P("fsdp"),P(d,None,None))
+    outs=(P(d,None,None),P(d,None,None),P(d),P(d),P(d,None),P(d),P(d),P(d,None),P(d),P(d),P(d),P(d,None),P(d),P(d,None),P(d))
+    def run(*args):
+        D,FF=args[11].shape; n=mesh.shape['fsdp']
+        local=args[0].shape[0]//mesh.size
+        whole=n%4==0 and mesh.shape['dp']==2 and D%(16*n)==0 and FF==4*D and local*args[0].shape[1]==D and D==64*HEADS and args[0].shape[1]%128==0
+        body=functools.partial(per_device,n//4) if whole else per_device_plain
+        return jax.shard_map(body,mesh=mesh,in_specs=ins,out_specs=outs,check_vma=False)(*args)
+    return run

time: 899 us -> 213 us (0.24)
  waiting for transfers between devices: 513 us -> 0 us
  Pallas kernels: 0 us -> 197 us
  matrix products: 151 us -> 0 us
  blocking collectives: 121 us -> 0 us
  other arithmetic: 45.9 us -> 3.36 us
  local copies, waits for them, and re-layouts: 45.2 us -> 12 us
  between operations: 17.6 us -> 0.77 us
    reduce_scatter x4 -> x0, waiting for transfers between devices: 365 us -> none  [the longest x1 142 us: per_device(): lax.psum_scatter(accum[9], ('fsdp', 'dp'), scatter_dimension=0, tiled=True)]
    pallas_call x0 -> x2, Pallas kernels: none -> 197 us  [the longest x1 106 us: k2_call(): pl.pallas_call(functools.partial(k2_body, D, FF, H, NZ, nseq, S), out_sha...]
    dot_general x72 -> x0, matrix products: 151 us -> none  [the longest x8 37.1 us: product_left_turned(): lax.dot_general(left_side, right_side, (((0,), (0,)), ((), ())), preferre...]
    all_gather x4 -> x0, waiting for transfers between devices: 145 us -> none  [the longest x1 74.9 us: per_device(): lax.all_gather(down_weight, 'fsdp', axis=0, tiled=True)]
    unnamed x2 -> x0, blocking collectives: 121 us -> none
    unnamed x390 -> x43, local copies, waits for them, and re-layouts: 28 us -> 11.3 us
    add x17 -> x0, other arithmetic: 14.5 us -> none  [the longest x9 9.64 us: per_device(): accum = [earlier + later for earlier, later in zip(accum, terms)]]
    reduce_sum x17 -> x0, other arithmetic: 12.1 us -> none  [the longest x8 3.64 us: attend_forward(): row_total = jnp.sum(exponent, axis=-1, keepdims=True)]
  transfers between devices with their start and end apart: 8 -> 0, of which waited for: 5 -> 0; matrix products, arithmetic and copies ran while one was open for 18% -> 0% of each run, Pallas kernels for 0% -> 0%
where the time goes in v1:
time: 213 us
  Pallas kernels  197 us (92%)
  local copies, waits for them, and re-layouts  12 us (6%)
  other arithmetic  3.36 us (2%)
    pallas_call x1, Pallas kernels, k2_call(): pl.pallas_call(functools.partial(k2_body, D, FF, H, NZ, nseq, S), out_sha...  106 us
    pallas_call x1, Pallas kernels, k1_call(): pl.pallas_call(functools.partial(k1_body, D, FF, H, NZ, nseq, S, 1), out_...  90.6 us
    unnamed x43, local copies, waits for them, and re-layouts  11.3 us

profile of v1, /device:TPU:0, one launch (start us, length us, event | category | flops | bytes accessed | tf_op | source)
XLA Modules:
  0.0 212.8 jit_solution(11742675864087422485)
XLA Ops:
  0.6 0.7 convert_element_type.24
  1.3 0.7 pad_convert_fusion.6
  2.0 0.7 pad_convert_fusion.4
  2.7 0.7 pad_convert_fusion.2
  3.3 0.7 pad_convert_fusion
  4.1 0.6 pad.74.refs_2_
  4.7 90.6 %gather_forward.1 = (bf16[768,768]{1,0:T(8,128)(2,1)}, bf16[2304,768]{1,0:T(8,128)(2,1)}, bf16[12,2,384,384]{3,2,1,0:T(8,128)(2,1)}, bf16[768,768]{1,0:T(8,128)(...) custom-call(bf16[768,768]{1,0:T(8,128)(2,1)} %bitcast.29, ...), custom_call_target="tpu_custom_call" | custom-call | tf_op jit(solution)/shard_map/gather_forward/pallas_call | solution.py:734
  95.3 106.0 %backward_scatter.1 = (f32[768,768]{1,0:T(8,128)}, f32[24,2304]{1,0:T(8,128)}, f32[24,768]{1,0:T(8,128)}, f32[24,3072]{1,0:T(8,128)}, f32[96,768]{1,0:T(8,128)},...) custom-call(bf16[3072,768]{1,0:T(8,128)(2,1)} %get-tuple-element.44., ...), custom_call_target="tpu_custom_call" | custom-call | tf_op jit(solution)/shard_map/backward_scatter/pallas_call | solution.py:989
  201.3 0.0 copy-start
  201.3 2.5 %copy.46 = bf16[2,384,768]{2,1,0:T(8,128)(2,1)} copy(bf16[2,384,768]{2,1,0:T(8,128)(2,1)} %bitcast.37) | data formatting | bytes 2359296
  203.8 0.0 copy-done
  203.9 0.0 copy-start.11
  204.0 1.4 copy.47
  205.4 0.5 copy.48
  205.9 0.5 copy.49
  206.4 0.7 copy.50
  207.1 0.5 copy.51
  207.6 0.0 copy-done.10
  207.6 0.5 copy.52
  208.1 0.0 copy-done.4
  208.1 0.6 copy.53
  208.7 0.5 copy.54
  209.3 0.5 copy.55
  209.8 0.0 copy-done.7
  209.8 0.5 copy.56
  210.3 0.0 copy-done.2
  210.3 0.7 copy.57
  211.0 0.0 copy-done.6
  211.0 0.5 copy.58
  211.5 0.7 copy.59
  212.2 0.0 copy-done.5
  212.2 0.5 copy.60
  (23 shorter events, 0.1 us)
Async XLA Ops:
  201.3 2.5 %copy-start = (f32[768,768]{1,0:T(8,128)S(1)}, f32[768,768]{1,0:T(8,128)}, u32[]{:S(2)}) copy-start(f32[768,768]{1,0:T(8,128)} %get-tuple-element.57) | copy-start | bytes 7077892
  203.8 1.5 copy-start.13
  203.8 2.0 copy-start.12
  203.8 2.5 %copy-start.3 = (f32[24,2304]{1,0:T(8,128)S(1)}, f32[24,2304]{1,0:T(8,128)}, u32[]{:S(2)}) copy-start(f32[24,2304]{1,0:T(8,128)} %get-tuple-element.98) | copy-start | bytes 663556
  203.9 3.2 %copy-start.11 = (f32[1,24]{1,0:T(1,128)S(1)}, f32[1,24]{1,0:T(1,128)}, u32[]{:S(2)}) copy-start(f32[1,24]{1,0:T(1,128)} %get-tuple-element.61) | copy-start | bytes 292
  203.9 3.7 %copy-start.10 = (f32[1,24]{1,0:T(1,128)S(1)}, f32[1,24]{1,0:T(1,128)}, u32[]{:S(2)}) copy-start(f32[1,24]{1,0:T(1,128)} %get-tuple-element.62) | copy-start | bytes 292
  203.9 4.2 %copy-start.4 = (f32[24,768]{1,0:T(8,128)S(1)}, f32[24,768]{1,0:T(8,128)}, u32[]{:S(2)}) copy-start(f32[24,768]{1,0:T(8,128)} %get-tuple-element.101) | copy-start | bytes 221188
  203.9 4.9 %copy-start.9 = (f32[1,24]{1,0:T(1,128)S(1)}, f32[1,24]{1,0:T(1,128)}, u32[]{:S(2)}) copy-start(f32[1,24]{1,0:T(1,128)} %get-tuple-element.64) | copy-start | bytes 292
  203.9 5.4 %copy-start.8 = (f32[1,24]{1,0:T(1,128)S(1)}, f32[1,24]{1,0:T(1,128)}, u32[]{:S(2)}) copy-start(f32[1,24]{1,0:T(1,128)} %get-tuple-element.65) | copy-start | bytes 292
  203.9 5.9 %copy-start.7 = (f32[1,24]{1,0:T(1,128)S(1)}, f32[1,24]{1,0:T(1,128)}, u32[]{:S(2)}) copy-start(f32[1,24]{1,0:T(1,128)} %get-tuple-element.66) | copy-start | bytes 292
  203.9 6.4 %copy-start.2 = (f32[24,3072]{1,0:T(8,128)S(1)}, f32[24,3072]{1,0:T(8,128)}, u32[]{:S(2)}) copy-start(f32[24,3072]{1,0:T(8,128)} %get-tuple-element.105) | copy-start | bytes 884740
  203.9 7.1 %copy-start.6 = (f32[1,96]{1,0:T(1,128)S(1)}, f32[1,96]{1,0:T(1,128)}, u32[]{:S(2)}) copy-start(f32[1,96]{1,0:T(1,128)} %get-tuple-element.68) | copy-start | bytes 1156
  203.9 7.6 %copy-start.1 = (f32[96,768]{1,0:T(8,128)S(1)}, f32[96,768]{1,0:T(8,128)}, u32[]{:S(2)}) copy-start(f32[96,768]{1,0:T(8,128)} %get-tuple-element.107) | copy-start | bytes 884740
  203.9 8.3 %copy-start.5 = (f32[1,24]{1,0:T(1,128)S(1)}, f32[1,24]{1,0:T(1,128)}, u32[]{:S(2)}) copy-start(f32[1,24]{1,0:T(1,128)} %get-tuple-element.70) | copy-start | bytes 292

commit v2 on v1

--- a/solution.py
+++ b/solution.py
@@ -500,9 +500,7 @@
         s.a1().start(); s.b1().start()
     def st2(s):
         s.a1().wait_recv(); s.b2().start()
-    def st3(s): s.b1().wait_recv()
-    def st4(s): s.b2().wait_recv()
-    def fin(s): pass
+    def fin(s): s.b1().wait_recv(); s.b2().wait_recv()
     def sent(s):
         others(s.pc, lambda z2: s.zc(z2).wait_send())
         s.a1().wait_send(); s.b1().wait_send(); s.b2().wait_send()
@@ -537,8 +535,9 @@
             def _(): s.dn(pc.z+d).start()
             s.corez(pc.z+d).start()
     def st3(s): s.relay(1)
-    def st4(s):
-        for d in range(2,s.pc.nz): s.relay(d)
+    def st4(s): s.relay(2)
+    def st5(s):
+        for d in range(3,s.pc.nz): s.relay(d)
     def sent(s):
         pc=s.pc
         for d in range(pc.nz):
@@ -571,15 +570,30 @@
     inv=lax.rsqrt(jnp.mean(cen*cen,axis=-1,keepdims=True)+EPS)
     return (cen*inv)*g+b
 
+PLAN_F={
+    'start':('V0', 'Q0', 'o0', 'd10', 'w0', 'u00', 'V1', 'd11', 'V2', 'u10', 'Vf', 'Q1', 'w1'),
+    'vec':('Q2', 'Q3'),
+    'n1':((1,('w2', 'd12', 'o1', 'w3', 'd00', 'Q4', 'u01')),(2,('Qf', 'w4', 'o2')),),
+    'qk':((0,('o3', 'wf')),),
+    'v':((0,('u11',)),),
+    'at':((0,('d13',)),(1,('u02', 'o4')),(4,('u12', 'u03')),(5,('of', 'd01')),),
+    'n2':((2,('u04',)),(5,('d14', 'u0f', 'u13')),),
+    'ul':((0,('u14', 'd02', 'u1f')),(1,('d15', 'd03')),),
+    'uh':((0,('d1f', 'd04')),(1,('d0f',)),),
+    'mask':(),
+}
+
 def chunks(D, FF, down_rows):
     h=down_rows//2
     return [(0,0,None,0,D,'M'),(0,0,None,2*D,D//2,'M'),(1,0,None,0,D//2,'M'),(2,0,None,0,FF//4,'M'),(2,0,None,FF//2,FF//4,'M'),(3,0,h,0,D//2,'M'),(3,h,h,0,D//2,'N')]
 
 def k1_body(D,FF,H,NZ,nseq,S,ev_lag, *refs):
-    (tok,segr,slab,wq,wo,wu,wd,
+    (tok,segr,*refs)=refs
+    vin=refs[:9]
+    (wq,wo,wu,wd,
      out_h,qkv_h,pt_h,att_h,hid_h,n1_h,n2_h,act_h,slp_h,gq_h,go_h,gu_h,gd_h,vec_h,
      gq,go,gu,gd,vbuf,n1,qkv,att,hid,n2,act,slp,outb,pst,bias,vec,upb,n1t,n2t,attt,actt,
-     zs,lsem,ss,so,loc,hsem,psem)=refs
+     slab,zs,lsem,ss,so,loc,hsem,psem)=refs[9:]
     R=nseq*S
     pc=Place(NZ)
     bufs=[gq,go,gu,gd]; ws=[wq,wo,wu,wd]
@@ -596,100 +610,92 @@
         cp=pltpu.make_async_copy(src, view(pc.z,pc.p,pc.c), loc.at[k]); cp.start(); own.append(cp)
     def vview(z,p,c):
         return vbuf.at[slice(None) if z is None else z, slice(None) if p is None else p]
+    slab[...]=jnp.zeros_like(slab)
+    for q in range(8): slab[q:q+1,:D//(4*NZ)]=vin[q][...].astype(F32)
+    slab[8:9,:]=vin[8][:,:128].astype(F32); slab[9:10,:FF//(4*NZ)-128]=vin[8][:,128:].astype(F32)
     kv=len(CH)
     gv=GatherVec(pc,kv,'V',vview,slab,zs,lsem,ss,so)
     cp=pltpu.make_async_copy(slab, vview(pc.z,pc.p,pc.c), loc.at[kv]); cp.start(); own.append(cp)
     barrier(pc)
-    gv.st0(); gs[0].st0()
-    gs[6].st0()
-    for k in range(1,6): gs[k].st0()
+    ev={}
+    for nm,g in zip(('Q','w','o','u0','u1','d0','d1','V'),gs+[gv]):
+        for st in '012345': ev[nm+st]=getattr(g,'st'+st,None)
+        ev[nm+'f']=g.fin
+    run=lambda name,n,body: loop(n,body,[(i,ev[e]) for i,es in PLAN_F.get(name,()) for e in es])
     for cp in own: cp.wait()
+    for e in PLAN_F['start']: ev[e]()
     sends=[]
     def put(src,dst,sem):
         c=pltpu.make_async_copy(src,dst,sem); c.start(); sends.append(c)
     for q in range(nseq):
         row=jnp.broadcast_to(segr[q:q+1,:],(S,S))
         bias[q]=jnp.where(row==row.T,0.0,-1e30).astype(F32)
-    gv.st1(); gs[0].st1(); gs[6].st1(); gs[1].st1()
-    gv.st2(); gv.st3(); gs[0].st2(); gs[0].st3(); gv.st4()
+    for e in PLAN_F['mask']: ev[e]()
     rows=[vbuf[i//4,i%4] for i in range(4*NZ)]
     nv=D//(4*NZ)
     vec[...]=jnp.concatenate([r[:,:nv] for r in rows],axis=1)
     upb[...]=jnp.concatenate([jnp.concatenate([r[8:9,:],r[9:10,:FF//(4*NZ)-128]],axis=1) for r in rows],axis=1)
-    gs[6].st2(); gs[1].st2(); gs[2].st1()
+    for e in PLAN_F['vec']: ev[e]()
     BR=128
     def n1b(i):
         r=pl.ds(pl.multiple_of(i*BR,BR),BR)
         y=norm(tok[r,:].astype(F32),vec[0:1,:],vec[1:2,:]).astype(BF)
         n1[r,:]=y
         n1t[:,r]=y.T
-    loop(R//BR,n1b)
-    gs[0].st4(); gs[1].st3(); gs[3].st1(); gs[2].st2()
+    run('n1',R//BR,n1b)
     put(n1t,n1_h,hsem.at[0]); put(vec,vec_h,hsem.at[1])
-    gs[0].fin()
     TN=256
     def qk(j):
-        c=pl.ds(pl.multiple_of(j*TN,TN),TN)
-        w=gq[:,:,:,c].reshape(D,TN)
-        y=dot(n1[...],w)
-        nq=D//TN
-        cb=pl.ds(pl.multiple_of((j%nq)*TN,TN),TN)
-        b=jnp.where(j<nq,vec[2:3,cb],jnp.where(j<2*nq,0.0,vec[3:4,cb]))
-        qkv[pl.ds(pl.multiple_of((j//nq)*R,128),R),cb]=(y+b).astype(BF)
-    loop(2*D//TN,qk)
-    gs[1].st4(); gs[2].st3(); gs[3].st2(); gs[4].st1()
-    gs[1].fin()
-    loop(D//TN,lambda j: qk(j+2*D//TN))
+        y=dot(n1[...],gq[:,:,:,pl.ds(pl.multiple_of(j*D,128),D)].reshape(D,D))
+        b=jnp.where(j==0,vec[2:3,:],jnp.where(j==1,0.0,vec[3:4,:]))
+        qkv[pl.ds(pl.multiple_of(j*R,128),R),:]=(y+b).astype(BF)
+    run('qk',2,qk)
+    run('v',1,lambda j: qk(2))
     put(qkv,qkv_h,hsem.at[3])
     put(gq,gq_h,hsem.at[4])
-    gs[2].st4()
     HP=H//2
     lane=lax.broadcasted_iota(jnp.int32,(1,128),1)
-    def attn(i):
+    def attn(i,sl):
         s=i//HP; hp=i%HP
         r=pl.ds(pl.multiple_of(s*S,128),S)
         hc=pl.ds(pl.multiple_of(hp*128,128),128)
         q2,k2,v2=[qkv[pl.ds(pl.multiple_of(w*R+s*S,128),S),hc] for w in range(3)]
         vT=v2.T
-        sl=i%2
         @pl.when(i>=2)
         def _(): pltpu.make_async_copy(pst.at[sl],pt_h.at[i-2],psem.at[sl]).wait()
-        os_=[]
-        for h in range(2):
-            qm=jnp.where((lane>=64) if h else (lane<64),q2*BF(0.125),BF(0))
-            sT=dotT(k2,qm)+bias[s]
-            m=jnp.max(sT,axis=0,keepdims=True)
-            e=jnp.exp(sT-m)
-            l=jnp.sum(e,axis=0,keepdims=True)
-            p=(e*(1.0/l)).astype(BF)
-            pst[sl,h]=p
-            os_.append(dot(vT[64*h:64*h+64],p))
-        oT=jnp.concatenate(os_,axis=0).astype(BF)
+        q=q2*BF(0.125)
+        km=jnp.concatenate([jnp.where(lane<64,k2,BF(0)),jnp.where(lane<64,BF(0),k2)],axis=0)
+        for x in range(0,S,128):
+            sc=dotT(km,q[x:x+128])
+            for h in range(2):
+                sT=sc[h*S:(h+1)*S]+bias[s,:,x:x+128]
+                m=jnp.max(sT,axis=0,keepdims=True)
+                e=jnp.exp(sT-m)
+                l=jnp.sum(e,axis=0,keepdims=True)
+                pst[sl,h,:,x:x+128]=(e*(1.0/l)).astype(BF)
+        oT=jnp.concatenate([dot(vT[64*h:64*h+64],pst[sl,h]) for h in range(2)],axis=0).astype(BF)
         attt[hc,r]=oT
         att[r,hc]=oT.T
         pltpu.make_async_copy(pst.at[sl],pt_h.at[i],psem.at[sl]).start()
-    loop(2*HP if nseq==2 else nseq*HP,attn,[(0,gs[3].st3),(1,gs[4].st2),(2,gs[5].st1),(4,gs[3].st4),(5,gs[6].st3),(6,gs[4].st3),(8,gs[5].st2),(9,gs[4].st4)])
+    def attn2(i):
+        for sl in range(2): attn(2*i+sl,sl)
+    run('at',nseq*HP//2,attn2)
     put(attt,att_h,hsem.at[5])
-    gs[2].fin()
     put(go,go_h,hsem.at[6])
     def op(j):
-        c=pl.ds(pl.multiple_of(j*TN,TN),TN)
-        w=go[:,:,:,c].reshape(D,TN)
-        hid[:,c]=dot(att[...],w)+vec[4:5,c]+tok[:,c].astype(F32)
-    loop(D//TN,op)
+        hid[...]=dot(att[...],go[...].reshape(D,D))+vec[4:5,:]+tok[...].astype(F32)
+    run('op',1,op)
     put(hid,hid_h,hsem.at[7])
-    gs[5].st3()
     def n2b(i):
         r=pl.ds(pl.multiple_of(i*BR,BR),BR)
         y=norm(hid[r,:],vec[5:6,:],vec[6:7,:]).astype(BF)
         n2[r,:]=y
         n2t[:,r]=y.T
-    loop(R//BR,n2b)
+    run('n2',R//BR,n2b)
     put(n2t,n2_h,hsem.at[8])
-    gs[3].fin()
     def upj(j):
-        c=pl.ds(pl.multiple_of(j*TN,TN),TN)
-        w=gu[:,:,:,c].reshape(D,TN)
+        c=pl.ds(pl.multiple_of(j*D,128),D)
+        w=gu[:,:,:,c].reshape(D,D)
         u=dot(n2[...],w)+upb[:,c]
         u2=u*u
         t=jnp.tanh(SLOPE*(u+CUBIC*u*u2))
@@ -698,18 +704,16 @@
         act[:,c]=a
         actt[c,:]=a.T
         slp[:,c]=(hp1+0.5*u*(1.0-t*t)*(SLOPE*(1.0+3.0*CUBIC*u2))).astype(BF)
-    loop(FF//2//TN,upj,[(2,gs[5].st4)])
-    gs[4].fin()
+    run('ul',FF//2//D,upj)
+    run('uh',FF//2//D,lambda j: upj(j+FF//2//D))
     put(gu,gu_h,hsem.at[9])
-    loop(FF//2//TN,lambda j: upj(j+FF//2//TN),[(2,gs[6].st4)])
     put(actt,act_h,hsem.at[10]); put(slp,slp_h,hsem.at[11])
-    gs[5].fin(); gs[6].fin()
     put(gd,gd_h,hsem.at[12])
     def dn(j):
         c=pl.ds(pl.multiple_of(j*TN,TN),TN)
         w=gd[:,:,:,c].reshape(FF,TN)
         outb[:,c]=(dot(act[...],w)+vec[7:8,c]+hid[:,c]).astype(BF)
-    loop(D//TN,dn)
+    run('dn',D//TN,dn)
     put(outb,out_h,hsem.at[13])
     n=nseq*HP
     for i in (n-2,n-1):
@@ -718,7 +722,7 @@
     gv.sent()
     for c in sends: c.wait()
 
-def k1_call(tok,segr,slab,wq,wo,wu,wd,D,FF,H,NZ):
+def k1_call(tok,segr,vs,wq,wo,wu,wd,D,FF,H,NZ):
     nseq,S=tok.shape[0],tok.shape[1]
     R=nseq*S
     sds=jax.ShapeDtypeStruct
@@ -728,20 +732,32 @@
     n=8
     scr=[V(g,BF) for g in g4]+[V((NZ,4,16,128),F32),V((R,D),BF),V((3*R,D),BF),V((R,D),BF),V((R,D),F32),V((R,D),BF),V((R,FF),BF),V((R,FF),BF),V((R,D),BF),V((2,2,S,S),BF),V((nseq,S,S),F32),V((16,D),F32),V((1,FF),F32),V((D,R),BF),V((D,R),BF),V((D,R),BF),V((FF,R),BF)]
     dma=pltpu.SemaphoreType.DMA
+    scr+=[V((16,128),F32)]
     scr+=[dma((n,NZ)),dma((n,7)),dma((n,NZ)),dma((n,7+NZ)),dma((n,)),dma((14,)),dma((2,))]
     vm=pl.BlockSpec(memory_space=pltpu.VMEM); anyb=pl.BlockSpec(memory_space=pl.ANY)
     flops=2*R*D*(4*D+2*FF)
     return pl.pallas_call(functools.partial(k1_body,D,FF,H,NZ,nseq,S,1),
-        out_shape=outs,in_specs=[vm]*7,out_specs=[anyb]*len(outs),scratch_shapes=scr,name="gather_forward",
+        out_shape=outs,in_specs=[vm]*15,out_specs=[anyb]*len(outs),scratch_shapes=scr,name="gather_forward",
         compiler_params=pltpu.CompilerParams(collective_id=0,has_side_effects=True,vmem_limit_bytes=63*1024*1024))(
-        tok.reshape(R,D),segr,slab,wq,wo,wu,wd)
-
-def make_slab(vs, upb):
-    m=vs[0].shape[0]; L=upb.shape[0]
-    rows=[jnp.pad(v.astype(F32)[None],((0,0),(0,128-m))) for v in vs]
-    u=upb.astype(F32)
-    rows.append(u[None,:128]); rows.append(jnp.pad(u[None,128:],((0,0),(0,256-L))))
-    return jnp.pad(jnp.concatenate(rows,axis=0),((0,6),(0,0)))
+        tok.reshape(R,D),segr,*[v[None] for v in vs],wq,wo,wu,wd)
+
+
+PLAN_B={
+    'l1':((7,('d0P',)),),
+    'l2':((0,('d1P', 'd0B')),(3,('d0A',)),),
+    'u0':((1,('d1B', 'u0P')),),
+    'u1':((1,('u1P',)),),
+    'l4':((1,('u1B',)),(2,('d1A',)),),
+    'l5':((5,('d0Z',)),),
+    'ow':((0,('u1A',)),),
+    'at0_':((0,('u0B',)),(1,('d1Z', 'oP')),),
+    'at1_':((0,('a0P', 'u1Z', 'a0B', 'u0A', 'oB')),),
+    'at2_':((0,('a1P', 'a0A')),),
+    'qw2_':((0,('a1B', 'u1F', 'u0Z')),),
+    'l9':((0,('oA', 'a2P')),(1,('a1A', 'a2B', 'a0Z')),),
+    'l10':((1,('oZ',)),),
+    'end':('u0F', 'vP', 'a2A', 'a1Z', 'vB', 'vA', 'a2Z', 'oF', 'd0F', 'd1F', 'vZ', 'a1F', 'a2F', 'a0F', 'vF'),
+}
 
 class Scatter:
     def __init__(s, pc, k, g, pb_, bb, ab, zb, out, sem, zsem, kv):
@@ -771,7 +787,7 @@
                 s.g[pc.c,z,p]=s.g[pc.c,z,p]+s.pb_[z,p]
                 return 0
             lax.fori_loop(0,pc.nz,add,0)
-        s.b(0).start(); s.b(1).start()
+        s.b(1).start(); s.b(0).start()
     def stA(s):
         pc=s.pc; s.b(1).wait_recv()
         def add(z,_):
@@ -785,11 +801,11 @@
             s.g[pc.c,z,pc.p]=(s.g[pc.c,z,pc.p].astype(F32)+s.pb_[z,pc.p].astype(F32)+(s.bb[0,z].astype(F32)+s.ab[z].astype(F32))).astype(s.g.dtype)
             return 0
         lax.fori_loop(0,pc.nz,add,0)
+        s.zb[pc.z]=s.g[pc.c,pc.z,pc.p]
         others(pc, lambda z2: s.zc(z2).start())
     def stF(s):
         pc=s.pc
         others(pc, lambda z2: s.zr(z2).wait_recv())
-        s.zb[pc.z]=s.g[pc.c,pc.z,pc.p]
         t=s.zb[0].astype(F32)
         for z in range(1,pc.nz): t=t+s.zb[z].astype(F32)
         s.out(t)
@@ -800,11 +816,11 @@
 def k2_body(D,FF,H,NZ,nseq,S,*refs):
     (actT_h,cot_h,gd_h,slp_h,n2T_h,gu_h,hid_h,attT_h,go_h,qkv_h,pt_h,gq_h,n1T_h,tok_h,vec_h,
      tg_h,o_q,o_o,o_u,o_d,*rest)=refs
-    o_v=rest[:9]
+    o_v=rest[0]
     (actT,cot,gd,slp,n2T,gu,hid,attT,go,vec,pst,dn,br,datt,dqkv,vg,ug,
-     gd0,gd1,*rest)=rest[9:]
-    (p0,p1,p2,p3,p4,p5,p6,b0,b1,b2,b3,b4,b5,b6,a0,a1,a2,a3,a4,a5,a6,z0,z1,z2,z3,z4,z5,z6,
-     gu0,gu1,gout,gv,vgb,vp,vb,va,vz,sem,zsem,lsem,psem,osem)=rest
+     gd0,gd1,*rest)=rest[1:]
+    ps,bs,as_,zs,rest=rest[:8],rest[8:16],rest[16:24],rest[24:32],rest[32:]
+    (gu0,gu1,gout,gv,vgb,vp,vb,va,vz,dsb,sem,zsem,lsem,psem,osem)=rest
     R=nseq*S
     pc=Place(NZ)
     qkv,n1T,gq,tok,gqk=actT.at[pl.ds(0,3*R)],actT.at[pl.ds(3*R,R)],gd,n2T,gd0
@@ -828,14 +844,22 @@
             ref[pl.ds(r0,t.shape[0]),pl.ds(c0,t.shape[1])]=t
         return fn
     HF=FF//2
-    sc=[Scatter(pc,0,gd0,p0,b0,a0,z0,outd(0),sem,zsem,0),
-        Scatter(pc,1,gd1,p1,b1,a1,z1,outd(rd//2),sem,zsem,0),
-        Scatter(pc,2,gu0,p2,b2,a2,z2,outw(o_u,0,0),sem,zsem,0),
-        Scatter(pc,3,gu1,p3,b3,a3,z3,outw(o_u,0,HF),sem,zsem,0),
-        Scatter(pc,4,gout,p4,b4,a4,z4,outw(o_o,0,0),sem,zsem,0),
-        Scatter(pc,5,gqk,p5,b5,a5,z5,outw(o_q,0,0),sem,zsem,0),
-        Scatter(pc,6,gv,p6,b6,a6,z6,outw(o_q,0,2*D),sem,zsem,0)]
+    def outa(n):
+        def fn(t):
+            for w in range(3): o_q[:,w*D+n*TN:w*D+(n+1)*TN]=t[:,w*TN:(w+1)*TN]
+        return fn
     TN=256
+    ng=D//TN
+    half=lambda w: gd0.at[:,:,:,:,pl.ds(w*D,D)]
+    ga=[half(0),half(1),gv]
+    names8=('d0','d1','u0','u1','o','a0','a1','a2')
+    gs8=(gd0,gd1,gu0,gu1,gout,*ga)
+    fo=(outd(0),outd(rd//2),outw(o_u,0,0),outw(o_u,0,HF),outw(o_o,0,0),outa(0),outa(1),outa(2))
+    sc={nm:Scatter(pc,i,gs8[i],ps[i],bs[i],as_[i],zs[i],fo[i],sem,zsem,0) for i,nm in enumerate(names8)}
+    ev={}
+    for nm in names8:
+        for st in 'PBAZF': ev[nm+st]=getattr(sc[nm],'st'+st)
+    run=lambda name,n,body: loop(n,body,[(i,ev[e]) for i,es in PLAN_B.get(name,()) for e in es])
     lanes=lambda j,w=TN: pl.ds(pl.multiple_of(j*w,128),w)
     vg[...]=jnp.zeros_like(vg)
     need(0,1)
@@ -846,34 +870,32 @@
                 for h,g in enumerate((gd0,gd1)):
                     o=(d*2+c)*rd+h*(rd//2)
                     for w in range(2): g[c,i//2,2*(i%2)+d,:,w*D:(w+1)*D]=y[o+w*rr:o+(w+1)*rr]
-    loop(2*NZ,l1)
-    sc[0].stP(); sc[1].stP()
+    run('l1',2*NZ,l1)
     fetch(9,11)
     need(2,3)
     def l2(j):
-        c=lanes(j)
-        da=dotT(cot[...],gd[pl.ds(pl.multiple_of(j*TN,TN),TN),:])
+        c=lanes(j,D)
+        da=dotT(cot[...],gd[pl.ds(pl.multiple_of(j*D,128),D),:])
         du=(da*slp[:,c].astype(F32)).astype(BF)
         slp[:,c]=du
         ug[:,c]=jnp.sum(du.astype(F32),axis=0,keepdims=True)
-    loop(FF//TN,l2,[(3,sc[0].stB),(6,sc[1].stB)])
+    run('l2',FF//D,l2)
     for c in gqc: c.start()
     need(4)
     def scat(g,lhs,rhs,rhs_c,g_c):
-        y=dot(lhs[...],rhs[:,rhs_c]).reshape(NZ,4,2,rr,TN)
+        w=g_c.size
+        y=dot(lhs[...],rhs[:,rhs_c]).reshape(NZ,4,2,rr,w)
         for c in range(2):
             for z in range(NZ):
                 g[c,z,:,:,g_c]=y[z,:,c].astype(BF)
-    nh=HF//TN
-    loop(nh,lambda j: scat(gu0,n2T,slp,lanes(j),lanes(j)),[(2,sc[0].stA)])
-    sc[2].stP()
-    loop(nh,lambda j: scat(gu1,n2T,slp,lanes(j+nh),lanes(j)),[(2,sc[1].stA),(3,sc[2].stB)])
-    sc[3].stP()
+    nh=HF//D
+    run('u0',nh,lambda j: scat(gu0,n2T,slp,lanes(j,D),lanes(j,D)))
+    run('u1',nh,lambda j: scat(gu1,n2T,slp,lanes(j+nh,D),lanes(j,D)))
     fetch(12)
     need(5)
     def l4(j):
         dn[:,lanes(j)]=dotT(slp[...],gu[pl.ds(pl.multiple_of(j*TN,TN),TN),:])
-    loop(D//TN,l4,[(0,sc[0].stZ),(1,sc[3].stB)])
+    run('l4',D//TN,l4)
     need(6,13)
     BR=128
     def back(x,g,gain,top):
@@ -894,79 +916,76 @@
         vg[5:6,:]+=gg; vg[6:7,:]+=gs
         vg[4:5,:]+=jnp.sum(hb.astype(F32),axis=0,keepdims=True)
         vg[7:8,:]+=jnp.sum(ct,axis=0,keepdims=True)
-    loop(R//BR,l5,[(2,sc[1].stZ),(4,sc[2].stA)])
+    run('l5',R//BR,l5)
     need(7,8)
-    loop(D//TN,lambda j: scat(gout,attT,br,lanes(j),lanes(j)),[(1,sc[0].stF)])
-    sc[4].stP()
+    run('ow',1,lambda j: scat(gout,attT,br,lanes(0,D),lanes(0,D)))
     def l6(j):
-        datt[:,lanes(j)]=dotT(br[...],go[pl.ds(pl.multiple_of(j*TN,TN),TN),:]).astype(BF)
-    loop(D//TN,l6,[(0,sc[3].stA),(1,sc[4].stB)])
+        datt[...]=dotT(br[...],go[...]).astype(BF)
+    run('l6',1,l6)
     need(9)
     HP=H//2
     n=nseq*HP
     lane=lax.broadcasted_iota(jnp.int32,(1,128),1)
-    pcopy=lambda i: pltpu.make_async_copy(pt_h.at[i],pst.at[i%2],psem.at[i%2])
-    pcopy(0).start()
-    def l7(i):
-        s=i//HP; hp=i%HP
+    pcopy=lambda i,sl: pltpu.make_async_copy(pt_h.at[(i%nseq)*HP+i//nseq],pst.at[sl],psem.at[sl])
+    pcopy(0,0).start(); pcopy(1,1).start()
+    def l7(i,sl):
+        s=i%nseq; hp=i//nseq
         r=pl.ds(pl.multiple_of(s*S,128),S)
         c0,c1,c2=[pl.ds(pl.multiple_of(w*D+hp*128,128),128) for w in range(3)]
-        pcopy(i).wait()
-        @pl.when(i+1<n)
-        def _(): pcopy(i+1).start()
+        pcopy(i,sl).wait()
         q2,k2,v2=[actT[pl.ds(pl.multiple_of(w*R+s*S,128),S),c0] for w in range(3)]; da=datt[r,c0]
         kT=k2.T
-        dq=[];dk=[];dv=[]
-        for h in range(2):
-            lo=(lane>=64) if h else (lane<64)
-            pT=pst[i%2,h]
-            dv.append(dot(pT,da))
-            dpT=dotT(v2,jnp.where(lo,da,BF(0)))
-            pf=pT.astype(F32)
-            t=dpT*pf
-            ds=(t-pf*jnp.sum(t,axis=0,keepdims=True)).astype(BF)
-            dk.append(dot(ds,q2))
-            dq.append(dot(kT[64*h:64*h+64],ds))
-        dvv=jnp.where(lane<64,dv[0],dv[1]).astype(BF)
-        dkk=(jnp.where(lane<64,dk[0],dk[1])*0.125).astype(BF)
+        vm=jnp.concatenate([jnp.where(lane<64,v2,BF(0)),jnp.where(lane<64,BF(0),v2)],axis=0)
+        for x in range(0,S,128):
+            dp=dotT(vm,da[x:x+128])
+            for h in range(2):
+                pf=pst[sl,h,:,x:x+128].astype(F32)
+                t=dp[h*S:(h+1)*S]*pf
+                dsb[h,:,x:x+128]=(t-pf*jnp.sum(t,axis=0,keepdims=True)).astype(BF)
+        dvb=dot(pst[sl].reshape(2*S,S),da)
+        dkb=dot(dsb[...].reshape(2*S,S),q2)
+        dvv=jnp.where(lane<64,dvb[:S],dvb[S:]).astype(BF)
+        dkk=(jnp.where(lane<64,dkb[:S],dkb[S:])*0.125).astype(BF)
+        dq=[dot(kT[64*h:64*h+64],dsb[h]) for h in range(2)]
         dqq=(jnp.concatenate(dq,axis=0).T*0.125).astype(BF)
         dqkv[r,c0]=dqq; dqkv[r,c1]=dkk; dqkv[r,c2]=dvv
         vg[2:3,c0]+=jnp.sum(dqq.astype(F32),axis=0,keepdims=True)
         vg[3:4,c0]+=jnp.sum(dvv.astype(F32),axis=0,keepdims=True)
-    loop(n,l7,[(1,sc[2].stZ),(2,sc[1].stF),(3,sc[4].stA),(5,sc[3].stZ),(6,sc[2].stF),(8,sc[4].stZ),(10,sc[3].stF),(11,sc[4].stF)])
+        @pl.when(i+2<n)
+        def _(): pcopy(i+2,sl).start()
+    def l7b(i):
+        for sl in range(2): l7(2*i+sl,sl)
     need(11)
-    sc[0].sent()
-    nq=D//TN
-    loop(2*nq,lambda j: scat(gqk,n1T,dqkv,lanes(j),lanes(j)))
-    sc[5].stP()
-    loop(nq,lambda j: scat(gv,n1T,dqkv,lanes(j+2*nq),lanes(j)),[(0,sc[5].stB)])
-    sc[6].stP()
+    per=n//ng//2
+    for g in range(ng):
+        run('at%d_'%g,per,lambda i,g=g: l7b(i+g*per))
+        if g==0: sc['d0'].sent()
+        def qw(i,g=g):
+            for w in range(3): scat(ga[g],n1T,dqkv,pl.ds(w*D+g*TN,TN),pl.ds(w*TN,TN))
+        run('qw%d_'%g,1,qw)
     for c in gqc: c.wait()
     need(12)
     def l9(j):
         dn[:,lanes(j)]=sum(dotT(dqkv[:,w*D:(w+1)*D],gq[pl.ds(pl.multiple_of(w*D+j*TN,TN),TN),:]) for w in range(3))
-    loop(nq,l9,[(0,sc[6].stB)])
+    run('l9',D//TN,l9)
     def l10(i):
         r=pl.ds(pl.multiple_of(i*BR,BR),BR)
         t,gg,gs=back(tok[r,:].astype(F32),dn[r,:],vec[0:1,:],hid[r,:])
         dn[r,:]=t
         vg[0:1,:]+=gg; vg[1:2,:]+=gs
-    loop(R//BR,l10,[(2,sc[5].stA)])
+    run('l10',R//BR,l10)
     oc=pltpu.make_async_copy(dn,tg_h,osem.at[0]); oc.start()
     nv=D//(4*NZ); nu=FF//(4*NZ)
     for i in range(4*NZ):
         for c in range(2):
             vgb[c,i//4,i%4]=jnp.concatenate([jnp.pad(vg[0:8,nv*i+c*(nv//2):nv*i+(c+1)*(nv//2)],((0,0),(0,128-nv//2))),
                jnp.pad(ug[:,nu*i+c*(nu//2):nu*i+(c+1)*(nu//2)],((0,7),(0,128-nu//2)))],axis=0)
-    def outv(t):
-        for q in range(8): o_v[q][...]=t[q:q+1,:nv//2]
-        o_v[8][...]=t[8:9,:nu//2]
-    sv=Scatter(pc,7,vgb,vp,vb,va,vz,outv,sem,zsem,0)
-    sv.stP()
-    sc[6].stA();
-    sv.stB(); sc[5].stZ(); sc[6].stZ(); sv.stA(); sv.stZ()
-    sc[5].stF(); sc[6].stF(); sv.stF()
-    for s in sc[1:]+[sv]: s.sent()
+    def outv(t): o_v[...]=t
+    sv=Scatter(pc,8,vgb,vp,vb,va,vz,outv,sem,zsem,0)
+    for st in 'PBAZF': ev['v'+st]=getattr(sv,'st'+st)
+    for e in PLAN_B['end']: ev[e]()
+    for nm in names8[1:]: sc[nm].sent()
+    sv.sent()
     oc.wait()
 
 def k2_call(sv,cot,tok,D,FF,H,NZ,S):
@@ -975,26 +994,53 @@
     sds=jax.ShapeDtypeStruct; V=pltpu.VMEM; dma=pltpu.SemaphoreType.DMA
     rr=D//(8*NZ); rd=FF//(8*NZ); nd=8*NZ
     ins=(actT,cot.reshape(R,D),gd.reshape(FF,D),slp,n2T,gu.reshape(D,FF),hid,attT,go.reshape(D,D),qkv,pt,gq.reshape(D,3*D),n1T,tok.reshape(R,D),vec)
-    outs=[sds((R,D),F32),sds((rr,3*D),F32),sds((rr,D),F32),sds((rr,FF),F32),sds((rd,D),F32)]+[sds((1,rr),F32)]*8+[sds((1,rd),F32)]
+    outs=[sds((R,D),F32),sds((rr,3*D),F32),sds((rr,D),F32),sds((rr,FF),F32),sds((rd,D),F32)]+[sds((16,128),F32)]
     vm=pl.BlockSpec(memory_space=pltpu.VMEM); anyb=pl.BlockSpec(memory_space=pl.ANY)
-    pieces=[(rr,FF//2),(rr,FF//2),(rr,FF//2),(rr,FF//2),(rr,D),(rr,2*D),(rr,D)]
+    pieces=[(rr,FF//2),(rr,FF//2),(rr,FF//2),(rr,FF//2),(rr,D),(rr,D),(rr,D),(rr,D)]
     scr=[V((FF,R),BF),V((R,D),BF),V((FF,D),BF),V((R,FF),BF),V((D,R),BF),V((D,FF),BF),V((R,D),F32),V((D,R),BF),V((D,D),BF),V((16,D),F32),
         V((2,2,S,S),BF),V((R,D),F32),V((R,D),BF),V((R,D),BF),V((R,3*D),BF),V((16,D),F32),V((1,FF),F32)]
     scr+=[V((2,NZ,4)+p,BF) for p in pieces[:2]]
     scr+=[V((NZ,4)+p,BF) for p in pieces]+[V((2,NZ)+p,BF) for p in pieces]+[V((NZ,)+p,BF) for p in pieces]+[V((NZ,)+p,BF) for p in pieces]
-    scr+=[V((2,NZ,4)+p,BF) for p in (pieces[2],pieces[3],pieces[4],pieces[6])]
+    scr+=[V((2,NZ,4)+p,BF) for p in (pieces[2],pieces[3],pieces[4],pieces[7])]
     vp=(16,128)
     scr+=[V((2,NZ,4)+vp,F32),V((NZ,4)+vp,F32),V((2,NZ)+vp,F32),V((NZ,)+vp,F32),V((NZ,)+vp,F32)]
-    scr+=[dma((8,2,4)),dma((8,2,NZ)),dma((17,)),dma((2,)),dma((1,))]
+    scr+=[V((2,S,S),BF)]
+    scr+=[dma((9,2,4)),dma((9,2,NZ)),dma((17,)),dma((2,)),dma((1,))]
     o=pl.pallas_call(functools.partial(k2_body,D,FF,H,NZ,nseq,S),out_shape=outs,in_specs=[anyb]*15,
         out_specs=[anyb]+[vm]*(len(outs)-1),scratch_shapes=scr,name="backward_scatter",
         compiler_params=pltpu.CompilerParams(collective_id=1,has_side_effects=True,vmem_limit_bytes=67043328))(*ins)
     return o
+
+def finish_body(D,FF,n,*refs):
+    k=2*n
+    ins=refs[:n]; small=refs[n]; outs=refs[n+1:k+1]; vecs=refs[k+1:k+10]; bufs=refs[k+10:k+10+n]; si,so=refs[k+10+n:]
+    cut=lambda i: [(o,ins[i].shape[0]//4) for o in range(0,ins[i].shape[0],ins[i].shape[0]//4)] if ins[i].shape[0]%64==0 else [(0,ins[i].shape[0])]
+    jobs=[]
+    for i in range(n):
+        for j,(o,w) in enumerate(cut(i)):
+            r=pl.ds(o,w)
+            a=pltpu.make_async_copy(ins[i].at[r],bufs[i].at[r],si.at[i,j])
+            a.start(); jobs.append((a,pltpu.make_async_copy(bufs[i].at[r],outs[i].at[r],so.at[i,j])))
+    t=small[...]
+    for q in range(9): vecs[q][...]=t[q:q+1,:vecs[q].shape[1]]
+    for a,b in jobs: a.wait(); b.start()
+    for a,b in jobs: b.wait()
+
+def finish_call(large,small,D,FF,nv,nu):
+    sds=jax.ShapeDtypeStruct; V=pltpu.VMEM; dma=pltpu.SemaphoreType.DMA
+    n=len(large)
+    vm=pl.BlockSpec(memory_space=pltpu.VMEM); anyb=pl.BlockSpec(memory_space=pl.ANY)
+    return pl.pallas_call(functools.partial(finish_body,D,FF,n),
+        out_shape=[sds(a.shape,a.dtype) for a in large]+[sds((1,nv),F32)]*8+[sds((1,nu),F32)],
+        in_specs=[anyb]*n+[vm],out_specs=[anyb]*n+[vm]*9,
+        scratch_shapes=[V(a.shape,a.dtype) for a in large]+[dma((n,4)),dma((n,4))],name="hand_out",
+        compiler_params=pltpu.CompilerParams(vmem_limit_bytes=67043328))(*large,small)
 def per_device(NZ,tokens,segments,first_gain,first_shift,qkv_weight,query_bias,value_bias,out_weight,out_bias,second_gain,second_shift,up_weight,up_bias,down_weight,down_bias,cotangent):
     D=tokens.shape[2]; FF=up_weight.shape[1]; S=tokens.shape[1]; H=HEADS
-    slab=make_slab((first_gain,first_shift,query_bias,value_bias,out_bias,second_gain,second_shift,down_bias),up_bias)
-    out,*sv=k1_call(tokens,segments,slab,qkv_weight,out_weight,up_weight,down_weight,D,FF,H,NZ)
-    tg,oq,oo,ou,od,*v=k2_call(sv,cotangent,tokens,D,FF,H,NZ,S)
+    vs=(first_gain,first_shift,query_bias,value_bias,out_bias,second_gain,second_shift,down_bias,up_bias)
+    out,*sv=k1_call(tokens,segments,vs,qkv_weight,out_weight,up_weight,down_weight,D,FF,H,NZ)
+    tg,oq,oo,ou,od,small=k2_call(sv,cotangent,tokens,D,FF,H,NZ,S)
+    out,tg,oq,oo,ou,od,*v=finish_call((out,tg,oq,oo,ou,od),small,D,FF,D//(8*NZ),FF//(8*NZ))
     v=[a.reshape(-1) for a in v]
     return (out.reshape(tokens.shape),tg.reshape(tokens.shape),v[0],v[1],oq,v[2],v[3],oo,v[4],v[5],v[6],ou,v[8],od,v[7])
 def specs_of(start):

time: 213 us -> 173 us (0.81)
  Pallas kernels: 197 us -> 170 us
  local copies, waits for them, and re-layouts: 12 us -> 1.22 us
  other arithmetic: 3.36 us -> 0 us
    pallas_call x1, Pallas kernels: 106 us -> 81.1 us  [k2_call(): pl.pallas_call(functools.partial(k2_body, D, FF, H, NZ, nseq, S), out_sha...]
    unnamed x43 -> x0, local copies, waits for them, and re-layouts: 11.3 us -> none
    pallas_call x1, Pallas kernels: 90.6 us -> 84 us  [k1_call(): pl.pallas_call(functools.partial(k1_body, D, FF, H, NZ, nseq, S, 1), out_...]
    pallas_call x0 -> x1, Pallas kernels: none -> 5.47 us  [finish_call(): pl.pallas_call(functools.partial(finish_body, D, FF, n), out_shape=[sds(a...]
    pad x4 -> x0, other arithmetic: 2.7 us -> none  [make_slab(): rows = [jnp.pad(v.astype(F32)[None], ((0, 0), (0, 128 - m))) for v in vs]]
where the time goes in v2:
time: 173 us
  Pallas kernels  170 us (98%)
    pallas_call x1, Pallas kernels, k1_call(): pl.pallas_call(functools.partial(k1_body, D, FF, H, NZ, nseq, S, 1), out_...  84 us
    pallas_call x1, Pallas kernels, k2_call(): pl.pallas_call(functools.partial(k2_body, D, FF, H, NZ, nseq, S), out_sha...  81.1 us
    pallas_call x1, Pallas kernels, finish_call(): pl.pallas_call(functools.partial(finish_body, D, FF, n), out_shape=[sds(a...  5.47 us

profile of v2, /device:TPU:0, one launch (start us, length us, event | category | flops | bytes accessed | tf_op | source)
XLA Modules:
  0.0 172.6 jit_solution(1193750871815231296)
XLA Ops:
  0.6 1.2 broadcast_in_dim.35.refs_10_
  1.9 84.0 %gather_forward.1 = (bf16[768,768]{1,0:T(8,128)(2,1)}, bf16[2304,768]{1,0:T(8,128)(2,1)}, bf16[12,2,384,384]{3,2,1,0:T(8,128)(2,1)}, bf16[768,768]{1,0:T(8,128)(...) custom-call(bf16[768,768]{1,0:T(8,128)(2,1)} %bitcast.25, ...), custom_call_target="tpu_custom_call" | custom-call | tf_op jit(solution)/shard_map/gather_forward/pallas_call | solution.py:739
  85.8 81.1 %backward_scatter.1 = (f32[768,768]{1,0:T(8,128)}, f32[24,2304]{1,0:T(8,128)}, f32[24,768]{1,0:T(8,128)}, f32[24,3072]{1,0:T(8,128)}, f32[96,768]{1,0:T(8,128)}, /*index=5*/f32[16,128]{1,0:T(8,128)}) custom-call(bf16[3072,768]{1,0:T(8,128)(2,1)} %get-tuple-element.51.refs_0_, bf16[768,768]{1,0:T(8,128)(2,1)} %bitcast.30, bf16[3072,768]{1,0:T(8,128)(2,1)} %bitcast.28, ...), custom_call_target="tpu_custom_call" | custom-call | tf_op jit(solution)/shard_map/backward_scatter/pallas_call | solution.py:1009
  166.9 5.5 %hand_out.1 = (bf16[768,768]{1,0:T(8,128)(2,1)}, f32[768,768]{1,0:T(8,128)}, f32[24,2304]{1,0:T(8,128)}, f32[24,768]{1,0:T(8,128)}, f32[24,3072]{1,0:T(8,128)}, ...) custom-call(bf16[768,768]{1,0:T(8,128)(2,1)} %get-tuple-element.50.r, ...), custom_call_target="tpu_custom_call" | custom-call | tf_op jit(solution)/shard_map/hand_out/pallas_call | solution.py:1033
